TPU v7x, 128 devices: a whole 4x4x4 slice. The times are simulated.
128 devices in a mesh: mom: 4 (over y), tm: 4 (over z_lo, core), pt: 8 (over x, z_hi).
Axes of the slice: x: 4, y: 4, z: 4 (z_hi: 2, z_lo: 2; z = z_hi * 2 + z_lo), core: 2. Of those that a mesh axis runs over, the one named last changes fastest.
Arguments:
- chi_time: bfloat16 [16, 8, 896, 896], P('tm', 'mom', 'pt'), may hold values from -4 to 4
- green: bfloat16 [8, 16, 896, 896], P('mom', 'tm', 'pt'), may hold values from -6 to 6
- band_coeffs: bfloat16 [896, 1024], replicated, may hold values from -1 to 1
Outputs:
- self_energy: float32 [8, 16, 1024], P('mom', 'tm', 'pt')
All inputs are finite; a program needn't handle non-finite values.
Results may differ from a plain program's by a relative error of at most 0.009.
Values may be sent and summed in bfloat16 or wider, within the bound.
No kernel may reach another device: no remote copies, remote signals or barrier semaphores. Data moves between devices by JAX's collectives and lax.ppermute only.
A program may use at most 64 MiB of HBM per device.

v0:
```python
import math

import jax
import jax.numpy as jnp
import numpy as np
from jax import lax
from jax.experimental import pallas as pl
from jax.experimental.pallas import tpu as pltpu
from jax.sharding import Mesh
from jax.sharding import PartitionSpec as P

COUPLING = 0.8
NT, NK, NP, NB = 16, 8, 896, 1024
GROUPS = 14

C5 = (math.sqrt(22.0) - 1.0) / 4.0
C3 = 0.75 - C5
C4 = 0.625
C6 = 2.0 - 1.25 * C5

TM = ("zlo", "core")
PLANE = ("x", "zhi", "zlo")
BY_ROWS = ("x", "zhi", "mom", "zlo", "core")
BY_OUTPUT = ("mom", "zlo", "core", "x", "zhi")


def exchange(pieces, axes):
    return lax.all_to_all(pieces, axes, split_axis=0, concat_axis=0, tiled=True)


def cosine_table(count):
    index = jnp.arange(count, dtype=jnp.float32) + 0.5
    angle = jnp.pi * index[:, None] * index[None, :] / count
    return (jnp.sqrt(jnp.float32(2.0 / count)) * jnp.cos(angle)).astype(jnp.bfloat16)


def to_frequency(cosine):
    eye = jnp.eye(8, dtype=jnp.bfloat16)
    return jnp.einsum("wt,ab->watb", cosine, eye).reshape(NT * 8, NT * 8)


def to_time(cosine):
    eye = jnp.eye(8, dtype=jnp.bfloat16)
    pair = jnp.eye(2, dtype=jnp.bfloat16)
    return jnp.einsum("tw,cd,ab->ctawdb", cosine, pair, eye).reshape(2 * NT * 8, NT * 2 * 8)


def frequency_kernel(times_ref, table_ref, out_ref):
    table = table_ref[...]
    scale = COUPLING / math.sqrt(NP)
    for group in range(7):
        rows = jnp.concatenate([times_ref[source, group] for source in range(4)], axis=0)
        mixed = jnp.dot(table, rows, preferred_element_type=jnp.float32) * scale
        out_ref[:, 8 * group : 8 * group + 8, :] = mixed.reshape(NT, 8, NP).astype(jnp.bfloat16)


def hartley8(x):
    root = math.sqrt(2.0)
    a0, a1, a2, a3 = x[0] + x[4], x[1] + x[5], x[2] + x[6], x[3] + x[7]
    b0, b1, b2, b3 = x[0] - x[4], x[1] - x[5], x[2] - x[6], x[3] - x[7]
    c0, c1, d0, d1 = a0 + a2, a1 + a3, a0 - a2, a1 - a3
    e0, e1, f1, f3 = b0 + b2, b0 - b2, root * b1, root * b3
    return [c0 + c1, e0 + f1, d0 + d1, e1 + f3, c0 - c1, e0 - f1, d0 - d1, e1 - f3]


def self_energy_kernel(screened_ref, table_ref, green_ref, coeffs_ref, own_ref, out_ref, time_ref, sigma_ref):
    table = table_ref[...]
    for mom in range(4):
        rows = jnp.concatenate([screened_ref[128 * p + 32 * mom : 128 * p + 32 * mom + 32, :] for p in range(8)], axis=0)
        time_ref[mom] = jnp.dot(table, rows, preferred_element_type=jnp.float32)
    norm = 1.0 / math.sqrt(NK)
    for pair in range(NT // 2):
        tiles = [time_ref[k // 2, 128 * (k % 2) + 16 * pair : 128 * (k % 2) + 16 * pair + 16, :] * norm for k in range(NK)]
        cells = hartley8(tiles)
        for r in range(NK):
            at = 256 * (r // 2) + 64 * (pair // 2) + 32 * (r % 2) + 16 * (pair % 2)
            value = green_ref[at : at + 16, :].astype(jnp.float32) * cells[r]
            sigma_ref[at : at + 16, :] = value.astype(jnp.bfloat16)
    own = own_ref[...].astype(jnp.float32)
    for block in range(4):
        applied = jnp.dot(sigma_ref[256 * block : 256 * block + 256, :], coeffs_ref[...], preferred_element_type=jnp.float32)
        values = jnp.sum(applied.reshape(32, 8, NB) * own[None], axis=1)
        for part in range(4):
            for p in range(8):
                out_ref[4 * block + part, p] = values[8 * part : 8 * part + 8, 128 * p : 128 * p + 128]


def local(chi_time, green, band_coeffs):
    cosine = cosine_table(NT)
    params = pltpu.CompilerParams(vmem_limit_bytes=40 * 1024 * 1024)

    e = (lax.axis_index("mom") * 2 + lax.axis_index("zlo")) * 2 + lax.axis_index("core")
    grouped = green.reshape(8, GROUPS, 8, NP).transpose(1, 0, 2, 3)
    grouped = jnp.concatenate([grouped, jnp.zeros((2, 8, 8, NP), jnp.bfloat16)], axis=0)
    cells = exchange(grouped, ("mom", "zlo", "core")).reshape(1024, NP)

    pieces = chi_time.reshape(4, 2, 2, 7, 8, NP).transpose(2, 1, 3, 0, 4, 5).reshape(4, 7, 32, NP)
    times = exchange(pieces, TM)
    mixed = pl.pallas_call(
        frequency_kernel, out_shape=jax.ShapeDtypeStruct((NT, 56, NP), jnp.bfloat16), compiler_params=params
    )(times, to_frequency(cosine))
    tile = exchange(mixed, PLANE).reshape(NP, NP)

    square = jnp.dot(tile, tile, preferred_element_type=jnp.float32).astype(jnp.bfloat16)
    wide, wide2 = tile.astype(jnp.float32), square.astype(jnp.float32)
    fourth = jnp.dot(square, (wide2 + 0.5 * wide).astype(jnp.bfloat16), preferred_element_type=jnp.float32)
    left = (fourth + C3 * wide2 + C4 * wide).astype(jnp.bfloat16)
    right = (fourth + C5 * wide2).astype(jnp.bfloat16)
    total = jnp.dot(left, right, preferred_element_type=jnp.float32) + C6 * fourth + wide2 + wide
    screened = total.astype(jnp.bfloat16).reshape(8, 112, NP)
    screened = jnp.concatenate([screened, jnp.zeros((8, 16, NP), jnp.bfloat16)], axis=1).reshape(128, 8, NP)
    spread = exchange(screened, BY_ROWS).reshape(1024, NP)

    row = (lax.axis_index("x") * 2 + lax.axis_index("zhi")) * 112 + 8 * e
    own = lax.dynamic_slice_in_dim(band_coeffs, row, 8, 0)
    partial_sums = pl.pallas_call(
        self_energy_kernel,
        out_shape=jax.ShapeDtypeStruct((16, 8, 8, 128), jnp.float32),
        scratch_shapes=[pltpu.VMEM((4, 256, NP), jnp.float32), pltpu.VMEM((1024, NP), jnp.bfloat16)],
        compiler_params=params,
    )(spread, to_time(cosine), cells, band_coeffs, own)
    shares = exchange(partial_sums.reshape(128, 8, 128), BY_OUTPUT)
    return shares.sum(axis=0).reshape(2, 4, 128)


def solution(mesh):
    fine = Mesh(mesh.devices.reshape(4, 2, 2, 4, 2), ("mom", "zlo", "core", "x", "zhi"))
    placed = (P(TM, "mom", ("x", "zhi"), None), P("mom", TM, ("x", "zhi"), None), P())
    return jax.shard_map(
        local, mesh=fine, in_specs=placed, out_specs=P("mom", TM, ("x", "zhi")), check_vma=False
    )
```

profile of v0, /device:TPU:1, one launch (start us, length us, event | category | flops | bytes accessed | tf_op | source)
XLA Modules:
  0.0 150.1 jit_solution(7557689084220345725)
XLA Ops:
  0.0 2.7 %copy.6 = bf16[4,2,2,7,8,896]{5,4,0,3,1,2:T(8,128)(2,1)} copy(bf16[4,2,2,7,8,896]{5,4,3,2,1,0:T(8,128)(2,1)} %bitcast.32) | data formatting | bytes 3211264 | tf_op jit(solution)/shard_map/reshape | solution.py:97
  2.7 5.0 %all-to-all-start = ((bf16[4,7,32,896]{3,2,1,0:T(8,128)(2,1)}), bf16[4,7,32,896]{3,2,1,0:T(8,128)(2,1)S(1)}, u32[]{:S(2)}, u32[]{:S(2)}) async-start(bf16[4,7,32,896]{3,2,1,0:T(8,128)(2,1)} %bitcast.2), calls=%async_computation | async-start | bytes 3211264 | tf_op jit(solution)/shard_map/all_to_all | solution.py:28
  7.7 0.1 multiply_convert_fusion
  7.8 0.1 copy.7
  7.9 0.1 multiply_bitcast_fusion.1
  8.0 0.5 reshape.48.table_ref
  8.5 18.7 %all-to-all-done.times_ref = bf16[4,7,32,896]{3,2,1,0:T(8,128)(2,1)S(1)} async-done(((bf16[4,7,32,896]{3,2,1,0:T(8,128)(2,1)}), bf16[4,7,32,896]{3,2,1,0:T(8,128)(2,1)S(1)}, u32[]{:S(2)}, u32[]{:S(2)}) %all-to-all-start) | async-done | bytes 1605664 | tf_op jit(solution)/shard_map/all_to_all | solution.py:28
  27.2 1.8 %shard_map.37 = bf16[16,56,896]{2,1,0:T(8,128)(2,1)} custom-call(bf16[4,7,32,896]{3,2,1,0:T(8,128)(2,1)S(1)} %all-to-all-done.times_ref, bf16[128,128]{1,0:T(8,128)(2,1)S(1)} %reshape.48.table_ref), custom_call_target="tpu_custom_call" | custom-call | tf_op jit(solution)/shard_map/pallas_call | solution.py:99
  29.0 0.0 copy-start.1
  29.0 7.7 %all-to-all-start.1 = ((bf16[16,56,896]{2,1,0:T(8,128)(2,1)}), bf16[16,56,896]{2,1,0:T(8,128)(2,1)}, u32[]{:S(2)}, u32[]{:S(2)}) async-start(bf16[16,56,896]{2,1,0:T(8,128)(2,1)} %shard_map.37), calls=%async_computation.1 | async-start | bytes 3211264 | tf_op jit(solution)/shard_map/all_to_all | solution.py:28
  36.7 0.0 copy-done.1
  36.7 0.2 copy.12
  37.0 1.5 concatenate.7
  38.5 19.2 %all-to-all-done.1 = bf16[16,56,896]{2,1,0:T(8,128)(2,1)} async-done(((bf16[16,56,896]{2,1,0:T(8,128)(2,1)}), bf16[16,56,896]{2,1,0:T(8,128)(2,1)}, u32[]{:S(2)}, u32[]{:S(2)}) %all-to-all-start.1) | async-done | bytes 1605664 | tf_op jit(solution)/shard_map/all_to_all | solution.py:28
  57.6 8.8 %all-to-all-start.3 = ((bf16[16,8,8,896]{3,2,1,0:T(8,128)(2,1)}), bf16[16,8,8,896]{3,2,1,0:T(8,128)(2,1)S(1)}, u32[]{:S(2)}, u32[]{:S(2)}) async-start(bf16[16,8,8,896]{3,2,1,0:T(8,128)(2,1)} %concatenate.7), calls=%async_computation.3 | async-start | bytes 3670016 | tf_op jit(solution)/shard_map/all_to_all | solution.py:28
  66.4 3.9 %fusion.21 = bf16[896,896]{1,0:T(8,128)(2,1)S(1)} fusion(bf16[896,896]{1,0:T(8,128)(2,1)} %bitcast.4), kind=kOutput, calls=%fused_computation.35 | convolution fusion | flops 1438646272 | bytes 3211264 | tf_op jit(solution)/shard_map/dot_general | solution.py:104
  70.3 3.5 %fusion.7 = f32[896,896]{1,0:T(8,128)S(1)} fusion(bf16[896,896]{1,0:T(8,128)(2,1)} %bitcast.4, bf16[896,896]{1,0:T(8,128)(2,1)S(1)} %fusion.21), kind=kOutput, calls=%fused_computation.14 | convolution fusion | flops 1442660352 | bytes 6422528 | tf_op jit(solution)/shard_map/dot_general | solution.py:106
  73.7 4.4 %fusion.2 = bf16[896,896]{1,0:T(8,128)(2,1)S(1)} fusion(bf16[896,896]{1,0:T(8,128)(2,1)} %bitcast.4, f32[896,896]{1,0:T(8,128)S(1)} %fusion.7, bf16[896,896]{1,0:T(8,128)(2,1)S(1)} %fusion.21), kind=kOutput, calls=%fused_computation.9 | convolution fusion | flops 1453096960 | bytes 8028160 | tf_op jit(solution)/shard_map/dot_general | solution.py:109
  78.2 1.5 concatenate.6
  79.7 10.9 %all-to-all-done.3 = bf16[16,8,8,896]{3,2,1,0:T(8,128)(2,1)S(1)} async-done(((bf16[16,8,8,896]{3,2,1,0:T(8,128)(2,1)}), bf16[16,8,8,896]{3,2,1,0:T(8,128)(2,1)S(1)}, u32[]{:S(2)}, u32[]{:S(2)}) %all-to-all-start.3) | async-done | bytes 1835040 | tf_op jit(solution)/shard_map/all_to_all | solution.py:28
  90.5 6.3 %all-to-all-start.2 = ((bf16[128,8,896]{2,1,0:T(8,128)(2,1)}), bf16[128,8,896]{2,1,0:T(8,128)(2,1)}, u32[]{:S(2)}, u32[]{:S(2)}) async-start(bf16[128,8,896]{2,1,0:T(8,128)(2,1)} %bitcast.30), calls=%async_computation.2 | async-start | bytes 3670016 | tf_op jit(solution)/shard_map/all_to_all | solution.py:28
  96.9 0.1 copy.8
  97.0 0.1 broadcast_multiply_fusion
  97.0 1.6 %multiply_bitcast_fusion = bf16[2,16,8,16,2,8]{2,1,0,5,4,3:T(8,128)(2,1)} fusion(bf16[16,16]{0,1:T(8,128)(2,1)S(1)} %multiply_convert_fusion, bf16[8,8,2,2]{0,2,1,3:T(2,128)(2,1)S(1)} %broadcast_multiply_fusion), kind=kLoop, calls=%fused_computation.16 | loop fusion | flops 65536 | bytes 132096 | tf_op jit(solution)/shard_map/tw,cd,ab->ctawdb/transpose | solution.py:45
  98.6 4.1 %reshape.53 = bf16[256,256]{0,1:T(8,128)(2,1)S(1)} reshape(bf16[2,16,8,16,2,8]{2,1,0,5,4,3:T(8,128)(2,1)} %multiply_bitcast_fusion) | data formatting | bytes 262144 | tf_op jit(solution)/shard_map/reshape | solution.py:45
  102.7 0.1 copy.10.table_ref
  102.8 0.7 constant_dynamic-slice_fusion.own_ref
  103.5 20.2 %all-to-all-done.2 = bf16[128,8,896]{2,1,0:T(8,128)(2,1)} async-done(((bf16[128,8,896]{2,1,0:T(8,128)(2,1)}), bf16[128,8,896]{2,1,0:T(8,128)(2,1)}, u32[]{:S(2)}, u32[]{:S(2)}) %all-to-all-start.2) | async-done | bytes 1835040 | tf_op jit(solution)/shard_map/all_to_all | solution.py:28
  123.7 1.5 copy-done
  125.2 5.8 %shard_map.38 = f32[16,8,8,128]{3,2,1,0:T(8,128)S(1)} custom-call(bf16[1024,896]{1,0:T(8,128)(2,1)} %bitcast.7.screened_ref, bf16[256,256]{1,0:T(8,128)(2,1)S(1)} %copy.10.table_ref, bf16[1024,896]{1,0:T(8,128)(2,1)S(1)} %bitcast.28, bf16[896,1024]{1,0:T(8,128)(2,1)S(1)} %copy-done, bf16[8,1024]{1,0:T(8,128)(2,1)S(1)} %constant_dynamic-slice_fusion.own_ref), custom_call_target="tpu_custom_call" | custom-call | tf_op jit(solution)/shard_map/pallas_call | solution.py:116
  131.0 18.4 %all_to_all.25 = f32[128,8,128]{2,1,0:T(8,128)S(1)} all-to-all(f32[128,8,128]{2,1,0:T(8,128)S(1)} %bitcast.29), channel_id=1, replica_groups=mesh['mom'=4,'zlo'=2,'core'=2,'x'=4,'zhi'=2] {'mom','zlo','core','x','zhi'}, dimensions={0} | all-to-all | bytes 1048576 | tf_op jit(solution)/shard_map/all_to_all | solution.py:28
  149.4 0.7 reduce_sum.9
  (4 shorter events, 0.0 us)
Async XLA Ops:
  2.7 24.5 %all-to-all-start = ((bf16[4,7,32,896]{3,2,1,0:T(8,128)(2,1)}), bf16[4,7,32,896]{3,2,1,0:T(8,128)(2,1)S(1)}, u32[]{:S(2)}, u32[]{:S(2)}) async-start(bf16[4,7,32,896]{3,2,1,0:T(8,128)(2,1)} %bitcast.2), calls=%async_computation | async-start | bytes 3211264 | tf_op jit(solution)/shard_map/all_to_all | solution.py:28
  29.0 7.7 %copy-start.1 = (bf16[2,4,112,896]{3,2,1,0:T(8,128)(2,1)S(1)}, bf16[2,4,112,896]{3,2,1,0:T(8,128)(2,1)}, u32[]{:S(2)}) copy-start(bf16[2,4,112,896]{3,2,1,0:T(8,128)(2,1)} %param.4) | copy-start | bytes 4816900
  29.0 28.6 %all-to-all-start.1 = ((bf16[16,56,896]{2,1,0:T(8,128)(2,1)}), bf16[16,56,896]{2,1,0:T(8,128)(2,1)}, u32[]{:S(2)}, u32[]{:S(2)}) async-start(bf16[16,56,896]{2,1,0:T(8,128)(2,1)} %shard_map.37), calls=%async_computation.1 | async-start | bytes 3211264 | tf_op jit(solution)/shard_map/all_to_all | solution.py:28
  57.6 32.9 %all-to-all-start.3 = ((bf16[16,8,8,896]{3,2,1,0:T(8,128)(2,1)}), bf16[16,8,8,896]{3,2,1,0:T(8,128)(2,1)S(1)}, u32[]{:S(2)}, u32[]{:S(2)}) async-start(bf16[16,8,8,896]{3,2,1,0:T(8,128)(2,1)} %concatenate.7), calls=%async_computation.3 | async-start | bytes 3670016 | tf_op jit(solution)/shard_map/all_to_all | solution.py:28
  90.5 33.2 %all-to-all-start.2 = ((bf16[128,8,896]{2,1,0:T(8,128)(2,1)}), bf16[128,8,896]{2,1,0:T(8,128)(2,1)}, u32[]{:S(2)}, u32[]{:S(2)}) async-start(bf16[128,8,896]{2,1,0:T(8,128)(2,1)} %bitcast.30), calls=%async_computation.2 | async-start | bytes 3670016 | tf_op jit(solution)/shard_map/all_to_all | solution.py:28
  123.7 1.5 copy-start
where the time goes:
time: 151 us; the launch traced here: 150 us
  waiting for transfers between devices  68.9 us (46%)
  starting transfers between devices  27.8 us (18%)
  blocking collectives  18.4 us (12%)
  local copies, waits for them, and re-layouts  12.9 us (9%)
  matrix products  11.8 us (8%)
  Pallas kernels  7.59 us (5%)
  other arithmetic  2.62 us (2%)
    all_to_all x4, waiting for transfers between devices, exchange(): return lax.all_to_all(pieces, axes, split_axis=0, concat_axis=0, tiled=True)  68.9 us
    all_to_all x4, starting transfers between devices, exchange(): return lax.all_to_all(pieces, axes, split_axis=0, concat_axis=0, tiled=True)  27.8 us
    all_to_all x1, blocking collectives, exchange(): return lax.all_to_all(pieces, axes, split_axis=0, concat_axis=0, tiled=True)  18.4 us
    pallas_call x1, Pallas kernels, local(): pl.pallas_call(self_energy_kernel, out_shape=jax.ShapeDtypeStruct((16, 8,...  5.81 us
    dot_general x1, matrix products, local(): jnp.dot(left, right, preferred_element_type=jnp.float32) + C6 * fourth  4.45 us
    reshape x2, local copies, waits for them, and re-layouts, to_time(): jnp.einsum('tw,cd,ab->ctawdb', cosine, pair, eye)  4.15 us
    dot_general x1, matrix products, local(): jnp.dot(tile, tile, preferred_element_type=jnp.float32).astype(jnp.bfloat16)  3.89 us
    dot_general x1, matrix products, local(): jnp.dot(square, (wide2 + 0.5 * wide).astype(jnp.bfloat16), preferred_elem...  3.46 us
  transfers between devices with their start and end apart: 4, of which 4 were waited for; matrix products, arithmetic and copies ran while one was open for 15% of the time, Pallas kernels for 0%

commit v1 on v0

v1 whole, which is shorter than its diff:
```python
import math

import jax
import jax.numpy as jnp
import ml_dtypes
import numpy as np
from jax import lax
from jax.experimental import pallas as pl
from jax.experimental.pallas import tpu as pltpu
from jax.sharding import Mesh
from jax.sharding import PartitionSpec as P

COUPLING = 0.8
NT, NK, NP, NB = 16, 8, 896, 1024
GROUPS = 14

C5 = (math.sqrt(22.0) - 1.0) / 4.0
C3 = 0.75 - C5
C4 = 0.625
C6 = 2.0 - 1.25 * C5

TM = ("zlo", "core")
PLANE = ("x", "zhi", "zlo")
BY_ROWS = ("x", "zhi", "mom", "zlo", "core")
BY_OUTPUT = ("mom", "zlo", "core", "x", "zhi")
MIB = 1024 * 1024


def exchange(pieces, axes):
    return lax.all_to_all(pieces, axes, split_axis=0, concat_axis=0, tiled=True)


def swap(piece, axes, step):
    return lax.ppermute(piece, axes, [(i, i ^ step) for i in range(4)])


def mixing_tables():
    index = np.arange(NT) + 0.5
    cosine = (np.sqrt(2.0 / NT) * np.cos(np.pi * index[:, None] * index[None, :] / NT)).astype(np.float32)
    wide, narrow, back = [], [], []
    for tm in range(4):
        times = [4 * ((place // 4) ^ tm) + place % 4 for place in range(NT)]
        wide.append(np.kron(cosine[:, times], np.eye(16)))
        narrow.append(np.kron(cosine[:, times], np.eye(8)))
        back.append(np.einsum("tw,cd,ab->ctawdb", cosine[times, :], np.eye(2), np.eye(8)).reshape(256, 256))
    return [np.stack(tables).astype(ml_dtypes.bfloat16) for tables in (wide, narrow, back)]


def frequency_kernel(own_ref, first_ref, second_ref, third_ref, wide_ref, narrow_ref, out_ref, mixed_ref, sent):
    pieces = (own_ref, first_ref, second_ref, third_ref)
    scale = COUPLING / math.sqrt(NP)
    sends = []

    def send(at, count):
        rows = pl.ds(at, count)
        sends.append(pltpu.make_async_copy(mixed_ref.at[:, rows], out_ref.at[:, rows], sent.at[len(sends)]))
        sends[-1].start()

    rows = jnp.concatenate([piece[t, 48:56, :].astype(jnp.float32) for piece in pieces for t in range(4)], axis=0)
    mixed = jnp.dot(narrow_ref[...], rows.astype(jnp.bfloat16), preferred_element_type=jnp.float32) * scale
    mixed_ref[:, 48:56, :] = mixed.reshape(NT, 8, NP).astype(jnp.bfloat16)
    send(48, 8)
    for at in range(0, 48, 16):
        rows = jnp.concatenate([piece[t, at : at + 16, :] for piece in pieces for t in range(4)], axis=0)
        mixed = jnp.dot(wide_ref[...], rows, preferred_element_type=jnp.float32) * scale
        mixed_ref[:, at : at + 16, :] = mixed.reshape(NT, 16, NP).astype(jnp.bfloat16)
        send(at, 16)
    for move in sends:
        move.wait()


def series_kernel(tile_ref, out_ref, square_ref, sum_ref, fourth_ref, left_ref, right_ref, padded_ref, sent):
    step = 224
    for at in range(0, NP, step):
        rows = slice(at, at + step)
        square = jnp.dot(tile_ref[rows, :], tile_ref[...], preferred_element_type=jnp.float32).astype(jnp.bfloat16)
        square_ref[rows, :] = square
        sum_ref[rows, :] = (square.astype(jnp.float32) + 0.5 * tile_ref[rows, :].astype(jnp.float32)).astype(jnp.bfloat16)
    for at in range(0, NP, step):
        rows = slice(at, at + step)
        fourth = jnp.dot(square_ref[rows, :], sum_ref[...], preferred_element_type=jnp.float32)
        square = square_ref[rows, :].astype(jnp.float32)
        tile = tile_ref[rows, :].astype(jnp.float32)
        left_ref[rows, :] = (fourth + C3 * square + C4 * tile).astype(jnp.bfloat16)
        right_ref[rows, :] = (fourth + C5 * square).astype(jnp.bfloat16)
        fourth_ref[rows, :] = C6 * fourth + square + tile
    for at in range(0, NP, step):
        rows = slice(at, at + step)
        total = jnp.dot(left_ref[rows, :], right_ref[...], preferred_element_type=jnp.float32) + fourth_ref[rows, :]
        total = total.astype(jnp.bfloat16)
        for half in range(2):
            to = 128 * (at // 112 + half)
            padded_ref[to : to + 96, :] = total[112 * half : 112 * half + 96]
            padded_ref[to + 96 : to + 112, :] = jnp.zeros((16, NP), jnp.bfloat16)
            padded_ref[to + 112 : to + 128, :] = total[112 * half + 96 : 112 * half + 112]
        rows = pl.ds(256 * (at // step), 256)
        pltpu.make_async_copy(padded_ref.at[rows], out_ref.at[rows], sent.at[at // step]).start()
    for block in range(4):
        rows = pl.ds(256 * block, 256)
        pltpu.make_async_copy(padded_ref.at[rows], out_ref.at[rows], sent.at[block]).wait()


def hartley8(x):
    root = math.sqrt(2.0)
    a0, a1, a2, a3 = x[0] + x[4], x[1] + x[5], x[2] + x[6], x[3] + x[7]
    b0, b1, b2, b3 = x[0] - x[4], x[1] - x[5], x[2] - x[6], x[3] - x[7]
    c0, c1, d0, d1 = a0 + a2, a1 + a3, a0 - a2, a1 - a3
    e0, e1, f1, f3 = b0 + b2, b0 - b2, root * b1, root * b3
    return [c0 + c1, e0 + f1, d0 + d1, e1 + f3, c0 - c1, e0 - f1, d0 - d1, e1 - f3]


def self_energy_kernel(place_ref, screened_ref, table_ref, *refs):
    cell_refs, (coeffs_ref, _, out_ref, time_ref, sigma_ref) = refs[:4], refs[4:]
    mom_here, tm_here = place_ref[0], place_ref[1]
    table = table_ref[...]
    for mom in range(4):
        rows = jnp.concatenate([screened_ref[128 * p + 32 * mom : 128 * p + 32 * mom + 32, :] for p in range(8)], axis=0)
        time_ref[mom] = jnp.dot(table, rows, preferred_element_type=jnp.float32)
    norm = 1.0 / math.sqrt(NK)
    own = coeffs_ref[NP:, :].astype(jnp.float32)
    for step in range(4):
        for pair in range(2):
            at = 32 * step + 16 * pair
            tiles = [time_ref[k // 2, 128 * (k % 2) + at : 128 * (k % 2) + at + 16, :] * norm for k in range(NK)]
            cells = hartley8(tiles)
            for r in range(NK):
                at = 32 * (r % 2) + 16 * pair
                value = cell_refs[step][(r // 2) ^ mom_here, at : at + 16, :].astype(jnp.float32) * cells[r]
                sigma_ref[step, 64 * (r // 2) + at : 64 * (r // 2) + at + 16, :] = value.astype(jnp.bfloat16)
        applied = jnp.dot(sigma_ref[step], coeffs_ref[:NP, :], preferred_element_type=jnp.float32)
        values = jnp.sum(applied.reshape(32, 8, NB) * own[None], axis=1)
        for mom in range(4):
            for p in range(8):
                share = values[8 * mom : 8 * mom + 8, 128 * p : 128 * p + 128]
                out_ref[4 * mom + (tm_here ^ step), p] = share.astype(out_ref.dtype)


def start_all(copies, done):
    moves = [pltpu.make_async_copy(source, target, done.at[i]) for i, (source, target) in enumerate(copies)]
    for move in moves:
        move.start()
    return moves


def copy_all(copies, done):
    for move in start_all(copies, done):
        move.wait()


def split_times_kernel(place_ref, chi_ref, *refs):
    targets = [place_ref[1] ^ step for step in range(4)]
    copies = [(chi_ref.at[t, target % 2, target // 2], refs[step].at[t]) for step, target in enumerate(targets) for t in range(4)]
    copy_all(copies, refs[4])


def split_rows_kernel(place_ref, green_ref, *refs):
    held, read, written = refs[4:]
    starts = [jnp.minimum(4 * (place_ref[0] ^ step), GROUPS - 4) for step in range(4)]
    moves = start_all([(green_ref.at[:, pl.ds(start, 4)], held.at[step]) for step, start in enumerate(starts)], read)
    for step, move in enumerate(moves):
        move.wait()
        pltpu.make_async_copy(held.at[step], refs[step], written.at[step]).start()
    for step in range(4):
        pltpu.make_async_copy(held.at[step], refs[step], written.at[step]).wait()


def split_groups_kernel(place_ref, *refs):
    held, read, written = refs[8:]
    copy_all([(refs[part].at[:, place_ref[1] ^ step], held.at[step, part]) for step in range(4) for part in range(4)], read)
    copy_all([(held.at[step], refs[4 + step]) for step in range(4)], written)


def arrived_kernel(*refs):
    refs[-1][...] = jnp.zeros((8, 128), jnp.float32)


ANY = pl.BlockSpec(memory_space=pl.ANY)
SMEM = pl.BlockSpec(memory_space=pltpu.SMEM)
VMEM = pl.BlockSpec(memory_space=pltpu.VMEM)
HBM = pl.BlockSpec(memory_space=pltpu.HBM)


def in_hbm(array):
    return pltpu.with_memory_space_constraint(array, pltpu.HBM)


def in_vmem(array):
    return pltpu.with_memory_space_constraint(array, pltpu.VMEM)


def copies_call(kernel, outs, space, inputs, scratch, cost=None):
    return pl.pallas_call(
        kernel,
        out_shape=outs,
        in_specs=[SMEM] + [ANY] * inputs,
        out_specs=[space] * len(outs),
        scratch_shapes=scratch,
        compiler_params=pltpu.CompilerParams(vmem_limit_bytes=4 * MIB),
        cost_estimate=cost,
    )


def sems(count):
    return pltpu.SemaphoreType.DMA((count,))


def local(chi_time, green, band_coeffs):
    mom = lax.axis_index("mom")
    tm = lax.axis_index("zlo") * 2 + lax.axis_index("core")
    place = jnp.stack([mom, tm]).astype(jnp.int32)
    wide, narrow, back = [lax.dynamic_index_in_dim(jnp.asarray(tables), tm, 0, False) for tables in mixing_tables()]
    vmem = lambda mib: pltpu.CompilerParams(vmem_limit_bytes=mib * MIB)
    long = pl.CostEstimate(flops=100000000000, transcendentals=0, bytes_accessed=4 * MIB)

    pieces = copies_call(split_times_kernel, [pltpu.VMEM((4, 56, NP), jnp.bfloat16)] * 4, VMEM, 1, [sems(16)])(place, in_hbm(chi_time.reshape(4, 2, 2, 56, NP)))
    received = [pieces[0]] + [swap(pieces[step], TM, step) for step in (1, 2, 3)]

    parts = copies_call(
        split_rows_kernel,
        [pltpu.HBM((8, 4, 8, NP), jnp.bfloat16)] * 4,
        HBM,
        1,
        [pltpu.VMEM((4, 8, 4, 8, NP), jnp.bfloat16), sems(4), sems(4)],
        cost=long,
    )(place, in_hbm(green.reshape(8, GROUPS, 8, NP)))
    by_mom = [parts[0]] + [swap(parts[step], "mom", step) for step in (1, 2, 3)]

    mixed = pl.pallas_call(
        frequency_kernel,
        out_shape=pltpu.HBM((NT, 56, NP), jnp.bfloat16),
        out_specs=HBM,
        scratch_shapes=[pltpu.VMEM((NT, 56, NP), jnp.bfloat16), sems(4)],
        compiler_params=vmem(8),
        cost_estimate=long,
    )(*received, wide, narrow)
    groups = copies_call(
        split_groups_kernel,
        [pltpu.HBM((4, 8, 8, NP), jnp.bfloat16)] * 4,
        HBM,
        4,
        [pltpu.VMEM((4, 4, 8, 8, NP), jnp.bfloat16), sems(16), sems(4)],
        cost=long,
    )(place, *by_mom)
    tile = exchange(mixed, PLANE).reshape(NP, NP)
    tile, groups = lax.optimization_barrier((tile, groups))
    cells = [groups[0]] + [swap(groups[step], TM, step) for step in (1, 2, 3)]
    cells = [cell.reshape(4, 64, NP) for cell in cells]
    arrived = pl.pallas_call(
        arrived_kernel, out_shape=jax.ShapeDtypeStruct((8, 128), jnp.float32), in_specs=[ANY] * 4, cost_estimate=long
    )(*cells)

    square = pltpu.VMEM((NP, NP), jnp.bfloat16)
    screened = pl.pallas_call(
        series_kernel,
        out_shape=pltpu.HBM((1024, NP), jnp.bfloat16),
        out_specs=HBM,
        scratch_shapes=[square, square, pltpu.VMEM((NP, NP), jnp.float32), square, square]
        + [pltpu.VMEM((1024, NP), jnp.bfloat16), pltpu.SemaphoreType.DMA((4,))],
        compiler_params=vmem(16),
        cost_estimate=long,
    )(tile)
    spread = exchange(screened.reshape(128, 8, NP), BY_ROWS).reshape(1024, NP)

    group = jnp.minimum(4 * mom, GROUPS - 4) + tm
    row = (lax.axis_index("x") * 2 + lax.axis_index("zhi")) * 112 + 8 * group
    own = lax.dynamic_slice_in_dim(band_coeffs, row, 8, 0)
    partial_sums = pl.pallas_call(
        self_energy_kernel,
        out_shape=jax.ShapeDtypeStruct((16, 8, 8, 128), jnp.bfloat16),
        in_specs=[SMEM] + [VMEM] * 8,
        scratch_shapes=[pltpu.VMEM((4, 256, NP), jnp.float32), pltpu.VMEM((4, 256, NP), jnp.bfloat16)],
        compiler_params=vmem(12),
    )(place, in_vmem(spread), back, *cells, jnp.concatenate([band_coeffs, own], axis=0), arrived)
    shares = exchange(partial_sums.reshape(128, 8, 128), BY_OUTPUT)
    return shares.astype(jnp.float32).sum(axis=0).reshape(2, 4, 128)


def solution(mesh):
    fine = Mesh(mesh.devices.reshape(4, 2, 2, 4, 2), ("mom", "zlo", "core", "x", "zhi"))
    placed = (P(TM, "mom", ("x", "zhi"), None), P("mom", TM, ("x", "zhi"), None), P())
    return jax.shard_map(
        local, mesh=fine, in_specs=placed, out_specs=P("mom", TM, ("x", "zhi")), check_vma=False
    )
```

time: 151 us -> 130 us (0.86)
  Pallas kernels: 7.59 us -> 26.2 us
  waiting for transfers between devices: 68.9 us -> 51.9 us
  matrix products: 11.8 us -> 0 us
  local copies, waits for them, and re-layouts: 12.9 us -> 5.73 us
  starting transfers between devices: 27.8 us -> 25 us
    all_to_all x4 -> x2, waiting for transfers between devices: 68.9 us -> 13.4 us  [exchange(): return lax.all_to_all(pieces, axes, split_axis=0, concat_axis=0, tiled=True)]
    ppermute x0 -> x9, waiting for transfers between devices: none -> 38.5 us  [swap(): return lax.ppermute(piece, axes, [(i, i ^ step) for i in range(4)])]
    pallas_call x1 -> x6, Pallas kernels: 1.78 us -> 19.7 us  [the longest x1 7.04 us: local(): pl.pallas_call(series_kernel, out_shape=pltpu.HBM((1024, NP), jnp.bfloat1...]
    all_to_all x4 -> x2, starting transfers between devices: 27.8 us -> 14.5 us  [exchange(): return lax.all_to_all(pieces, axes, split_axis=0, concat_axis=0, tiled=True)]
    dot_general x3 -> x0, matrix products: 11.8 us -> none  [the longest x1 4.45 us: local(): jnp.dot(left, right, preferred_element_type=jnp.float32) + C6 * fourth]
    ppermute x0 -> x9, starting transfers between devices: none -> 10.6 us  [swap(): return lax.ppermute(piece, axes, [(i, i ^ step) for i in range(4)])]
    reshape x5 -> x0, local copies, waits for them, and re-layouts: 7.6 us -> none  [the longest x2 4.15 us: to_time(): jnp.einsum('tw,cd,ab->ctawdb', cosine, pair, eye)]
    squeeze x0 -> x3, local copies, waits for them, and re-layouts: none -> 3.24 us  [local(): lax.dynamic_index_in_dim(jnp.asarray(tables), tm, 0, False)]
  transfers between devices with their start and end apart: 4 -> 11, of which waited for: 4 -> 5; matrix products, arithmetic and copies ran while one was open for 15% -> 4% of each run, Pallas kernels for 0% -> 13%
where the time goes in v1:
time: 130 us; the launch traced here: 129 us
  waiting for transfers between devices  51.9 us (40%)
  Pallas kernels  26.2 us (20%)
  starting transfers between devices  25 us (19%)
  blocking collectives  18 us (14%)
  local copies, waits for them, and re-layouts  5.73 us (4%)
  other arithmetic  2.45 us (2%)
    ppermute x9, waiting for transfers between devices, swap(): return lax.ppermute(piece, axes, [(i, i ^ step) for i in range(4)])  38.5 us
    all_to_all x1, blocking collectives, exchange(): return lax.all_to_all(pieces, axes, split_axis=0, concat_axis=0, tiled=True)  18 us
    all_to_all x2, starting transfers between devices, exchange(): return lax.all_to_all(pieces, axes, split_axis=0, concat_axis=0, tiled=True)  14.5 us
    all_to_all x2, waiting for transfers between devices, exchange(): return lax.all_to_all(pieces, axes, split_axis=0, concat_axis=0, tiled=True)  13.4 us
    ppermute x9, starting transfers between devices, swap(): return lax.ppermute(piece, axes, [(i, i ^ step) for i in range(4)])  10.6 us
    pallas_call x1, Pallas kernels, local(): pl.pallas_call(series_kernel, out_shape=pltpu.HBM((1024, NP), jnp.bfloat1...  7.04 us
    pallas_call x1, Pallas kernels, local(): pl.pallas_call(self_energy_kernel, out_shape=jax.ShapeDtypeStruct((16, 8,...  6.48 us
    pallas_call x1, Pallas kernels, local(): copies_call(split_groups_kernel, [pltpu.HBM((4, 8, 8, NP), jnp.bfloat16)]...  3.41 us
  transfers between devices with their start and end apart: 11, of which 5 were waited for; matrix products, arithmetic and copies ran while one was open for 4% of the time, Pallas kernels for 13%

profile of v1, /device:TPU:1, one launch (start us, length us, event | category | flops | bytes accessed | tf_op | source)
XLA Modules:
  0.0 129.4 jit_solution(16003080409343068269)
XLA Ops:
  0.0 0.1 pad_add_fusion.place_ref
  0.1 3.1 %shard_map.64 = (bf16[4,56,896]{2,1,0:T(8,128)(2,1)S(1)}, bf16[4,56,896]{2,1,0:T(8,128)(2,1)}, bf16[4,56,896]{2,1,0:T(8,128)(2,1)}, bf16[4,56,896]{2,1,0:T(8,128)(2,1)S(1)}) custom-call(s32[2]{0:T(128)S(1)} %pad_add_fusion.place_ref, bf16[4,2,2,56,896]{4,3,2,1,0:T(8,128)(2,1)} %bitcast.24), custom_call_target="tpu_custom_call" | custom-call | tf_op jit(solution)/shard_map/pallas_call | solution.py:215
  3.2 1.5 %collective-permute-start = (bf16[4,56,896]{2,1,0:T(8,128)(2,1)}, bf16[4,56,896]{2,1,0:T(8,128)(2,1)S(1)}, u32[]{:S(2)}, u32[]{:S(2)}) collective-permute-start(bf16[4,56,896]{2,1,0:T(8,128)(2,1)} %get-tuple-element.23), channel_id=1, source_target_pairs={{0,8},{8,0},{16,24},{24,16},{1,9},{9,1},{17,25},{25,17},{2,10},{10... | collective-permute-start | bytes 1204232 | tf_op jit(solution)/shard_map/ppermute | solution.py:34
  4.7 1.7 %collective-permute-start.1 = (bf16[4,56,896]{2,1,0:T(8,128)(2,1)}, bf16[4,56,896]{2,1,0:T(8,128)(2,1)}, u32[]{:S(2)}, u32[]{:S(2)}) collective-permute-start(bf16[4,56,896]{2,1,0:T(8,128)(2,1)} %get-tuple-element.24), channel_id=1, source_target_pairs={{0,16},{8,24},{16,0},{24,8},{1,17},{9,25},{17,1},{25,9},{2,18},{10... | collective-permute-start | bytes 1204232 | tf_op jit(solution)/shard_map/ppermute | solution.py:34
  6.5 2.9 %shard_map.66 = (bf16[8,4,8,896]{3,2,1,0:T(8,128)(2,1)}, bf16[8,4,8,896]{3,2,1,0:T(8,128)(2,1)}, bf16[8,4,8,896]{3,2,1,0:T(8,128)(2,1)}, bf16[8,4,8,896]{3,2,1,0:T(8,128)(2,1)}) custom-call(s32[2]{0:T(128)S(1)} %pad_add_fusion.place_ref, bf16[8,14,8,896]{3,2,1,0:T(8,128)(2,1)} %bitcast.25), custom_call_target="tpu_custom_call" | custom-call | flops 99999997952 | bytes 4194304 | tf_op jit(solution)/shard_map/pallas_call | solution.py:218
  9.4 1.4 %collective-permute-start.3 = (bf16[8,4,8,896]{3,2,1,0:T(8,128)(2,1)}, bf16[8,4,8,896]{3,2,1,0:T(8,128)(2,1)}, u32[]{:S(2)}, u32[]{:S(2)}) collective-permute-start(bf16[8,4,8,896]{3,2,1,0:T(8,128)(2,1)} %get-tuple-element.27), channel_id=1, source_target_pairs={{0,32},{32,0},{64,96},{96,64},{1,33},{33,1},{65,97},{97,65},{2,34}... | collective-permute-start | bytes 1376264 | tf_op jit(solution)/shard_map/ppermute | solution.py:34
  10.8 2.6 %collective-permute-start.4 = (bf16[8,4,8,896]{3,2,1,0:T(8,128)(2,1)}, bf16[8,4,8,896]{3,2,1,0:T(8,128)(2,1)}, u32[]{:S(2)}, u32[]{:S(2)}) collective-permute-start(bf16[8,4,8,896]{3,2,1,0:T(8,128)(2,1)} %get-tuple-element.28), channel_id=1, source_target_pairs={{0,64},{32,96},{64,0},{96,32},{1,65},{33,97},{65,1},{97,33},{2,66}... | collective-permute-start | bytes 1376264 | tf_op jit(solution)/shard_map/ppermute | solution.py:34
  13.4 0.8 dynamic-slice_bitcast_fusion.2.narrow_ref
  14.1 0.7 constant_dynamic-slice_fusion
  14.9 0.9 dynamic-slice_bitcast_fusion.1.wide_ref
  15.8 1.6 %dynamic-slice_bitcast_fusion.table_ref = bf16[256,256]{1,0:T(8,128)(2,1)} fusion(bf16[4,256,256]{2,1,0:T(8,128)(2,1)} %constant.53.clone, s32[]{:T(128)S(6)} %select_n.10), kind=kLoop, calls=%fused_computation.2 | loop fusion | bytes 262148 | tf_op jit(solution)/shard_map/jit(dynamic_index_in_dim)/squeeze | solution.py:211
  17.3 1.6 %pad_maximum_fusion.refs_4_ = bf16[904,1024]{1,0:T(8,128)(2,1)S(1)} fusion(bf16[8,1024]{1,0:T(8,128)(2,1)S(1)} %constant_dynamic-slice_fusion, bf16[896,1024]{1,0:T(8,128)(2,1)} %param.8), kind=kLoop, calls=%fused_computation | loop fusion | flops 3702784 | bytes 3702784 | tf_op jit(solution)/shard_map/concatenate | solution.py:273
  19.0 0.1 collective-permute-start.5
  19.1 6.1 %collective-permute-done.2.third_ref = bf16[4,56,896]{2,1,0:T(8,128)(2,1)} collective-permute-done((bf16[4,56,896]{2,1,0:T(8,128)(2,1)S(1)}, bf16[4,56,896]{2,1,0:T(8,128)(2,1)}, u32[]{:S(2)}, u32[]{:S(2)}) %collective-permute-start.2) | collective-permute-done | bytes 401440 | tf_op jit(solution)/shard_map/ppermute | solution.py:34
  25.2 2.7 %shard_map.65 = bf16[16,56,896]{2,1,0:T(8,128)(2,1)} custom-call(bf16[4,56,896]{2,1,0:T(8,128)(2,1)S(1)} %get-tuple-element.22.own_ref, bf16[4,56,896]{2,1,0:T(8,128)(2,1)S(1)} %collective-permute-done.first_ref, bf16[4,56,896]{2,1,0:T(8,128)(2,1)} %collective-permute-done.1.second_ref, bf16[4,56,896]{2,1,0:T(8,128)(2,1)} %collective-permute-done.2.third_ref, ...), custom_call_target="tpu_custom_call" | custom-call | flops 99999997952 | bytes 4194304 | tf_op jit(solution)/shard_map/pallas_call | solution.py:228
  27.8 7.4 %all-to-all-start = ((bf16[16,56,896]{2,1,0:T(8,128)(2,1)}), bf16[16,56,896]{2,1,0:T(8,128)(2,1)S(1)}, u32[]{:S(2)}, u32[]{:S(2)}) async-start(bf16[16,56,896]{2,1,0:T(8,128)(2,1)} %shard_map.65), calls=%async_computation | async-start | bytes 3211264 | tf_op jit(solution)/shard_map/all_to_all | solution.py:30
  35.3 6.6 %collective-permute-done.5.refs_3_ = bf16[8,4,8,896]{3,2,1,0:T(8,128)(2,1)} collective-permute-done((bf16[8,4,8,896]{3,2,1,0:T(8,128)(2,1)}, bf16[8,4,8,896]{3,2,1,0:T(8,128)(2,1)}, u32[]{:S(2)}, u32[]{:S(2)}) %collective-permute-start.5) | collective-permute-done | bytes 458784 | tf_op jit(solution)/shard_map/ppermute | solution.py:34
  41.9 1.0 copy-done.3
  42.9 3.4 %shard_map.67 = (bf16[4,8,8,896]{3,2,1,0:T(8,128)(2,1)}, bf16[4,8,8,896]{3,2,1,0:T(8,128)(2,1)}, bf16[4,8,8,896]{3,2,1,0:T(8,128)(2,1)}, bf16[4,8,8,896]{3,2,1,0:T(8,128)(2,1)}) custom-call(s32[2]{0:T(128)S(1)} %pad_add_fusion.place_ref, bf16[8,4,8,896]{3,2,1,0:T(8,128)(2,1)S(1)} %copy-done.3, bf16[8,4,8,896]{3,2,1,0:T(8,128)(2,1)} %collective-permute-done.3.refs_1_, ...), custom_call_target="tpu_custom_call" | custom-call | flops 99999997952 | bytes 4194304 | tf_op jit(solution)/shard_map/pallas_call | solution.py:236
  46.3 13.0 %all-to-all-done = bf16[16,56,896]{2,1,0:T(8,128)(2,1)S(1)} async-done(((bf16[16,56,896]{2,1,0:T(8,128)(2,1)}), bf16[16,56,896]{2,1,0:T(8,128)(2,1)S(1)}, u32[]{:S(2)}, u32[]{:S(2)}) %all-to-all-start) | async-done | bytes 1605664 | tf_op jit(solution)/shard_map/all_to_all | solution.py:30
  59.3 1.5 %collective-permute-start.6 = (bf16[4,8,8,896]{3,2,1,0:T(8,128)(2,1)}, bf16[4,8,8,896]{3,2,1,0:T(8,128)(2,1)}, u32[]{:S(2)}, u32[]{:S(2)}) collective-permute-start(bf16[4,8,8,896]{3,2,1,0:T(8,128)(2,1)} %get-tuple-element.36), channel_id=1, source_target_pairs={{0,8},{8,0},{16,24},{24,16},{1,9},{9,1},{17,25},{25,17},{2,10},{10... | collective-permute-start | bytes 1376264 | tf_op jit(solution)/shard_map/ppermute | solution.py:34
  60.9 0.5 collective-permute-start.7
  61.4 1.1 collective-permute-start.8
  62.5 7.0 %shard_map.68 = bf16[1024,896]{1,0:T(8,128)(2,1)} custom-call(bf16[896,896]{1,0:T(8,128)(2,1)S(1)} %bitcast.19), custom_call_target="tpu_custom_call" | custom-call | flops 99999997952 | bytes 4194304 | tf_op jit(solution)/shard_map/pallas_call | solution.py:253
  69.5 7.0 %all-to-all-start.1 = ((bf16[128,8,896]{2,1,0:T(8,128)(2,1)}), bf16[128,8,896]{2,1,0:T(8,128)(2,1)}, u32[]{:S(2)}, u32[]{:S(2)}) async-start(bf16[128,8,896]{2,1,0:T(8,128)(2,1)} %bitcast.23), calls=%async_computation.1 | async-start | bytes 3670016 | tf_op jit(solution)/shard_map/all_to_all | solution.py:30
  76.6 25.8 %collective-permute-done.8 = bf16[4,8,8,896]{3,2,1,0:T(8,128)(2,1)} collective-permute-done((bf16[4,8,8,896]{3,2,1,0:T(8,128)(2,1)}, bf16[4,8,8,896]{3,2,1,0:T(8,128)(2,1)}, u32[]{:S(2)}, u32[]{:S(2)}) %collective-permute-start.8) | collective-permute-done | bytes 458784 | tf_op jit(solution)/shard_map/ppermute | solution.py:34
  102.4 0.6 shard_map.69.refs_5_
  103.0 0.4 all-to-all-done.1
  103.5 0.7 copy-done.2
  104.1 6.5 %shard_map.70 = bf16[16,8,8,128]{3,2,1,0:T(8,128)(2,1)S(1)} custom-call(s32[2]{0:T(128)S(1)} %pad_add_fusion.place_ref, bf16[1024,896]{1,0:T(8,128)(2,1)} %bitcast.8.screened_ref, bf16[256,256]{1,0:T(8,128)(2,1)S(1)} %copy-done, bf16[4,64,896]{2,1,0:T(8,128)(2,1)S(1)} %bitcast.22, bf16[4,64,896]{2,1,0:T(8,128)(2,1)} %bitcast.11.refs_1_, ...), custom_call_target="tpu_custom_call" | custom-call | tf_op jit(solution)/shard_map/pallas_call | solution.py:267
  110.6 18.0 %all_to_all.15 = bf16[128,8,128]{2,1,0:T(8,128)(2,1)S(1)} all-to-all(bf16[128,8,128]{2,1,0:T(8,128)(2,1)S(1)} %bitcast.20), channel_id=1, replica_groups=mesh['mom'=4,'zlo'=2,'core'=2,'x'=4,'zhi'=2] {'mom','zlo','core','x','zhi'}, dimensions={0} | all-to-all | bytes 524288 | tf_op jit(solution)/shard_map/all_to_all | solution.py:30
  128.7 0.7 convert_reduce_fusion
  (13 shorter events, 0.1 us)
Async XLA Ops:
  3.2 15.8 %collective-permute-start = (bf16[4,56,896]{2,1,0:T(8,128)(2,1)}, bf16[4,56,896]{2,1,0:T(8,128)(2,1)S(1)}, u32[]{:S(2)}, u32[]{:S(2)}) collective-permute-start(bf16[4,56,896]{2,1,0:T(8,128)(2,1)} %get-tuple-element.23), channel_id=1, source_target_pairs={{0,8},{8,0},{16,24},{24,16},{1,9},{9,1},{17,25},{25,17},{2,10},{10... | collective-permute-start | bytes 1204232 | tf_op jit(solution)/shard_map/ppermute | solution.py:34
  4.7 14.4 %collective-permute-start.1 = (bf16[4,56,896]{2,1,0:T(8,128)(2,1)}, bf16[4,56,896]{2,1,0:T(8,128)(2,1)}, u32[]{:S(2)}, u32[]{:S(2)}) collective-permute-start(bf16[4,56,896]{2,1,0:T(8,128)(2,1)} %get-tuple-element.24), channel_id=1, source_target_pairs={{0,16},{8,24},{16,0},{24,8},{1,17},{9,25},{17,1},{25,9},{2,18},{10... | collective-permute-start | bytes 1204232 | tf_op jit(solution)/shard_map/ppermute | solution.py:34
  6.4 18.8 %collective-permute-start.2 = (bf16[4,56,896]{2,1,0:T(8,128)(2,1)S(1)}, bf16[4,56,896]{2,1,0:T(8,128)(2,1)}, u32[]{:S(2)}, u32[]{:S(2)}) collective-permute-start(bf16[4,56,896]{2,1,0:T(8,128)(2,1)S(1)} %get-tuple-element.25), channel_id=1, source_target_pairs={{0,24},{8,16},{16,8},{24,0},{1,25},{9,17},{17,9},{25,1},{2,26},{10... | collective-permute-start | bytes 1204232 | tf_op jit(solution)/shard_map/ppermute | solution.py:34
  9.4 25.9 %collective-permute-start.3 = (bf16[8,4,8,896]{3,2,1,0:T(8,128)(2,1)}, bf16[8,4,8,896]{3,2,1,0:T(8,128)(2,1)}, u32[]{:S(2)}, u32[]{:S(2)}) collective-permute-start(bf16[8,4,8,896]{3,2,1,0:T(8,128)(2,1)} %get-tuple-element.27), channel_id=1, source_target_pairs={{0,32},{32,0},{64,96},{96,64},{1,33},{33,1},{65,97},{97,65},{2,34}... | collective-permute-start | bytes 1376264 | tf_op jit(solution)/shard_map/ppermute | solution.py:34
  10.8 24.5 %collective-permute-start.4 = (bf16[8,4,8,896]{3,2,1,0:T(8,128)(2,1)}, bf16[8,4,8,896]{3,2,1,0:T(8,128)(2,1)}, u32[]{:S(2)}, u32[]{:S(2)}) collective-permute-start(bf16[8,4,8,896]{3,2,1,0:T(8,128)(2,1)} %get-tuple-element.28), channel_id=1, source_target_pairs={{0,64},{32,96},{64,0},{96,32},{1,65},{33,97},{65,1},{97,33},{2,66}... | collective-permute-start | bytes 1376264 | tf_op jit(solution)/shard_map/ppermute | solution.py:34
  19.0 22.9 %collective-permute-start.5 = (bf16[8,4,8,896]{3,2,1,0:T(8,128)(2,1)}, bf16[8,4,8,896]{3,2,1,0:T(8,128)(2,1)}, u32[]{:S(2)}, u32[]{:S(2)}) collective-permute-start(bf16[8,4,8,896]{3,2,1,0:T(8,128)(2,1)} %get-tuple-element.29), channel_id=1, source_target_pairs={{0,96},{32,64},{64,32},{96,0},{1,97},{33,65},{65,33},{97,1},{2,98}... | collective-permute-start | bytes 1376264 | tf_op jit(solution)/shard_map/ppermute | solution.py:34
  27.8 31.5 %all-to-all-start = ((bf16[16,56,896]{2,1,0:T(8,128)(2,1)}), bf16[16,56,896]{2,1,0:T(8,128)(2,1)S(1)}, u32[]{:S(2)}, u32[]{:S(2)}) async-start(bf16[16,56,896]{2,1,0:T(8,128)(2,1)} %shard_map.65), calls=%async_computation | async-start | bytes 3211264 | tf_op jit(solution)/shard_map/all_to_all | solution.py:30
  41.9 1.0 copy-start.3
  59.3 17.3 %collective-permute-start.6 = (bf16[4,8,8,896]{3,2,1,0:T(8,128)(2,1)}, bf16[4,8,8,896]{3,2,1,0:T(8,128)(2,1)}, u32[]{:S(2)}, u32[]{:S(2)}) collective-permute-start(bf16[4,8,8,896]{3,2,1,0:T(8,128)(2,1)} %get-tuple-element.36), channel_id=1, source_target_pairs={{0,8},{8,0},{16,24},{24,16},{1,9},{9,1},{17,25},{25,17},{2,10},{10... | collective-permute-start | bytes 1376264 | tf_op jit(solution)/shard_map/ppermute | solution.py:34
  60.9 15.7 %collective-permute-start.7 = (bf16[4,8,8,896]{3,2,1,0:T(8,128)(2,1)}, bf16[4,8,8,896]{3,2,1,0:T(8,128)(2,1)}, u32[]{:S(2)}, u32[]{:S(2)}) collective-permute-start(bf16[4,8,8,896]{3,2,1,0:T(8,128)(2,1)} %get-tuple-element.37), channel_id=1, source_target_pairs={{0,16},{8,24},{16,0},{24,8},{1,17},{9,25},{17,1},{25,9},{2,18},{10... | collective-permute-start | bytes 1376264 | tf_op jit(solution)/shard_map/ppermute | solution.py:34
  61.4 41.0 %collective-permute-start.8 = (bf16[4,8,8,896]{3,2,1,0:T(8,128)(2,1)}, bf16[4,8,8,896]{3,2,1,0:T(8,128)(2,1)}, u32[]{:S(2)}, u32[]{:S(2)}) collective-permute-start(bf16[4,8,8,896]{3,2,1,0:T(8,128)(2,1)} %get-tuple-element.38), channel_id=1, source_target_pairs={{0,24},{8,16},{16,8},{24,0},{1,25},{9,17},{17,9},{25,1},{2,26},{10... | collective-permute-start | bytes 1376264 | tf_op jit(solution)/shard_map/ppermute | solution.py:34
  69.5 33.9 %all-to-all-start.1 = ((bf16[128,8,896]{2,1,0:T(8,128)(2,1)}), bf16[128,8,896]{2,1,0:T(8,128)(2,1)}, u32[]{:S(2)}, u32[]{:S(2)}) async-start(bf16[128,8,896]{2,1,0:T(8,128)(2,1)} %bitcast.23), calls=%async_computation.1 | async-start | bytes 3670016 | tf_op jit(solution)/shard_map/all_to_all | solution.py:30
  102.4 1.0 copy-start
  102.4 1.1 copy-start.1
  103.5 0.7 copy-start.2

commit v2 on v1

--- a/solution.py
+++ b/solution.py
@@ -49,24 +49,14 @@
 def frequency_kernel(own_ref, first_ref, second_ref, third_ref, wide_ref, narrow_ref, out_ref, mixed_ref, sent):
     pieces = (own_ref, first_ref, second_ref, third_ref)
     scale = COUPLING / math.sqrt(NP)
-    sends = []
-
-    def send(at, count):
-        rows = pl.ds(at, count)
-        sends.append(pltpu.make_async_copy(mixed_ref.at[:, rows], out_ref.at[:, rows], sent.at[len(sends)]))
-        sends[-1].start()
-
     rows = jnp.concatenate([piece[t, 48:56, :].astype(jnp.float32) for piece in pieces for t in range(4)], axis=0)
     mixed = jnp.dot(narrow_ref[...], rows.astype(jnp.bfloat16), preferred_element_type=jnp.float32) * scale
     mixed_ref[:, 48:56, :] = mixed.reshape(NT, 8, NP).astype(jnp.bfloat16)
-    send(48, 8)
     for at in range(0, 48, 16):
         rows = jnp.concatenate([piece[t, at : at + 16, :] for piece in pieces for t in range(4)], axis=0)
         mixed = jnp.dot(wide_ref[...], rows, preferred_element_type=jnp.float32) * scale
         mixed_ref[:, at : at + 16, :] = mixed.reshape(NT, 16, NP).astype(jnp.bfloat16)
-        send(at, 16)
-    for move in sends:
-        move.wait()
+    copy_all([(mixed_ref.at[pl.ds(4 * i, 4)], out_ref.at[pl.ds(4 * i, 4)]) for i in range(4)], sent)
 
 
 def series_kernel(tile_ref, out_ref, square_ref, sum_ref, fourth_ref, left_ref, right_ref, padded_ref, sent):
@@ -84,20 +74,21 @@
         left_ref[rows, :] = (fourth + C3 * square + C4 * tile).astype(jnp.bfloat16)
         right_ref[rows, :] = (fourth + C5 * square).astype(jnp.bfloat16)
         fourth_ref[rows, :] = C6 * fourth + square + tile
-    for at in range(0, NP, step):
-        rows = slice(at, at + step)
+    sends = []
+    for at, count in (0, 224), (224, 224), (448, 224), (672, 112), (784, 112):
+        rows = slice(at, at + count)
         total = jnp.dot(left_ref[rows, :], right_ref[...], preferred_element_type=jnp.float32) + fourth_ref[rows, :]
         total = total.astype(jnp.bfloat16)
-        for half in range(2):
+        for half in range(count // 112):
             to = 128 * (at // 112 + half)
             padded_ref[to : to + 96, :] = total[112 * half : 112 * half + 96]
             padded_ref[to + 96 : to + 112, :] = jnp.zeros((16, NP), jnp.bfloat16)
             padded_ref[to + 112 : to + 128, :] = total[112 * half + 96 : 112 * half + 112]
-        rows = pl.ds(256 * (at // step), 256)
-        pltpu.make_async_copy(padded_ref.at[rows], out_ref.at[rows], sent.at[at // step]).start()
-    for block in range(4):
-        rows = pl.ds(256 * block, 256)
-        pltpu.make_async_copy(padded_ref.at[rows], out_ref.at[rows], sent.at[block]).wait()
+        rows = pl.ds(128 * (at // 112), 128 * (count // 112))
+        sends.append(pltpu.make_async_copy(padded_ref.at[rows], out_ref.at[rows], sent.at[len(sends)]))
+        sends[-1].start()
+    for send in sends:
+        send.wait()
 
 
 def hartley8(x):
@@ -110,15 +101,20 @@
 
 
 def self_energy_kernel(place_ref, screened_ref, table_ref, *refs):
-    cell_refs, (coeffs_ref, _, out_ref, time_ref, sigma_ref) = refs[:4], refs[4:]
+    cell_refs, (coeffs_hbm, own_ref, _, out_ref, time_ref, sigma_ref, coeffs_ref, held_ref, fetched) = list(refs[:4]), refs[4:]
+    parts = [pl.ds(448 * i, 448) for i in range(2)]
+    moves = start_all([(coeffs_hbm.at[part], coeffs_ref.at[part]) for part in parts] + [(cell_refs[0], held_ref)], fetched)
+    cell_refs[0] = held_ref
     mom_here, tm_here = place_ref[0], place_ref[1]
     table = table_ref[...]
     for mom in range(4):
         rows = jnp.concatenate([screened_ref[128 * p + 32 * mom : 128 * p + 32 * mom + 32, :] for p in range(8)], axis=0)
         time_ref[mom] = jnp.dot(table, rows, preferred_element_type=jnp.float32)
     norm = 1.0 / math.sqrt(NK)
-    own = coeffs_ref[NP:, :].astype(jnp.float32)
-    for step in range(4):
+    own = own_ref[...].astype(jnp.float32)
+    for step in (1, 2, 3, 0):
+        if step == 0:
+            moves[2].wait()
         for pair in range(2):
             at = 32 * step + 16 * pair
             tiles = [time_ref[k // 2, 128 * (k % 2) + at : 128 * (k % 2) + at + 16, :] * norm for k in range(NK)]
@@ -127,7 +123,10 @@
                 at = 32 * (r % 2) + 16 * pair
                 value = cell_refs[step][(r // 2) ^ mom_here, at : at + 16, :].astype(jnp.float32) * cells[r]
                 sigma_ref[step, 64 * (r // 2) + at : 64 * (r // 2) + at + 16, :] = value.astype(jnp.bfloat16)
-        applied = jnp.dot(sigma_ref[step], coeffs_ref[:NP, :], preferred_element_type=jnp.float32)
+        if step == 1:
+            for move in moves[:2]:
+                move.wait()
+        applied = jnp.dot(sigma_ref[step], coeffs_ref[...], preferred_element_type=jnp.float32)
         values = jnp.sum(applied.reshape(32, 8, NB) * own[None], axis=1)
         for mom in range(4):
             for p in range(8):
@@ -148,9 +147,18 @@
 
 
 def split_times_kernel(place_ref, chi_ref, *refs):
-    targets = [place_ref[1] ^ step for step in range(4)]
-    copies = [(chi_ref.at[t, target % 2, target // 2], refs[step].at[t]) for step, target in enumerate(targets) for t in range(4)]
-    copy_all(copies, refs[4])
+    held, read, written = refs[4:]
+    order = (3, 2, 1, 0)
+    targets = [place_ref[1] ^ step for step in order]
+    into = [refs[0] if step == 0 else held.at[step - 1] for step in order]
+    reads = start_all([(chi_ref.at[:, target % 2, target // 2], to) for target, to in zip(targets, into)], read)
+    writes = []
+    for step, move in zip(order, reads):
+        move.wait()
+        if step:
+            writes += start_all([(held.at[step - 1], refs[step])], written.at[pl.ds(step, 1)])
+    for move in writes:
+        move.wait()
 
 
 def split_rows_kernel(place_ref, green_ref, *refs):
@@ -212,7 +220,15 @@
     vmem = lambda mib: pltpu.CompilerParams(vmem_limit_bytes=mib * MIB)
     long = pl.CostEstimate(flops=100000000000, transcendentals=0, bytes_accessed=4 * MIB)
 
-    pieces = copies_call(split_times_kernel, [pltpu.VMEM((4, 56, NP), jnp.bfloat16)] * 4, VMEM, 1, [sems(16)])(place, in_hbm(chi_time.reshape(4, 2, 2, 56, NP)))
+    quarter = (4, 56, NP)
+    pieces = pl.pallas_call(
+        split_times_kernel,
+        out_shape=[jax.ShapeDtypeStruct(quarter, jnp.bfloat16)] + [pltpu.HBM(quarter, jnp.bfloat16)] * 3,
+        in_specs=[SMEM, HBM],
+        out_specs=[VMEM] + [HBM] * 3,
+        scratch_shapes=[pltpu.VMEM((3, *quarter), jnp.bfloat16), sems(4), sems(4)],
+        compiler_params=vmem(4),
+    )(place, in_hbm(chi_time.reshape(4, 2, 2, 56, NP)))
     received = [pieces[0]] + [swap(pieces[step], TM, step) for step in (1, 2, 3)]
 
     parts = copies_call(
@@ -246,8 +262,12 @@
     cells = [groups[0]] + [swap(groups[step], TM, step) for step in (1, 2, 3)]
     cells = [cell.reshape(4, 64, NP) for cell in cells]
     arrived = pl.pallas_call(
-        arrived_kernel, out_shape=jax.ShapeDtypeStruct((8, 128), jnp.float32), in_specs=[ANY] * 4, cost_estimate=long
-    )(*cells)
+        arrived_kernel,
+        out_shape=jax.ShapeDtypeStruct((8, 128), jnp.float32),
+        in_specs=[VMEM] * 2,
+        compiler_params=vmem(1),
+        cost_estimate=long,
+    )(*cells[2:])
 
     square = pltpu.VMEM((NP, NP), jnp.bfloat16)
     screened = pl.pallas_call(
@@ -255,7 +275,7 @@
         out_shape=pltpu.HBM((1024, NP), jnp.bfloat16),
         out_specs=HBM,
         scratch_shapes=[square, square, pltpu.VMEM((NP, NP), jnp.float32), square, square]
-        + [pltpu.VMEM((1024, NP), jnp.bfloat16), pltpu.SemaphoreType.DMA((4,))],
+        + [pltpu.VMEM((1024, NP), jnp.bfloat16), sems(5)],
         compiler_params=vmem(16),
         cost_estimate=long,
     )(tile)
@@ -267,10 +287,11 @@
     partial_sums = pl.pallas_call(
         self_energy_kernel,
         out_shape=jax.ShapeDtypeStruct((16, 8, 8, 128), jnp.bfloat16),
-        in_specs=[SMEM] + [VMEM] * 8,
-        scratch_shapes=[pltpu.VMEM((4, 256, NP), jnp.float32), pltpu.VMEM((4, 256, NP), jnp.bfloat16)],
+        in_specs=[SMEM, VMEM, VMEM, HBM, VMEM, VMEM, VMEM, HBM, VMEM, HBM],
+        scratch_shapes=[pltpu.VMEM((4, 256, NP), jnp.float32), pltpu.VMEM((4, 256, NP), jnp.bfloat16)]
+        + [pltpu.VMEM((NP, NB), jnp.bfloat16), pltpu.VMEM((4, 64, NP), jnp.bfloat16), sems(3)],
         compiler_params=vmem(12),
-    )(place, in_vmem(spread), back, *cells, jnp.concatenate([band_coeffs, own], axis=0), arrived)
+    )(place, in_vmem(spread), back, in_hbm(cells[0]), *cells[1:], in_hbm(band_coeffs), own, in_hbm(arrived))
     shares = exchange(partial_sums.reshape(128, 8, 128), BY_OUTPUT)
     return shares.astype(jnp.float32).sum(axis=0).reshape(2, 4, 128)
 

time: 130 us -> 126 us (0.969)
  Pallas kernels: 26.2 us -> 23.5 us
  other arithmetic: 2.45 us -> 0.8 us
  waiting for transfers between devices: 51.9 us -> 53.4 us
    all_to_all x2, waiting for transfers between devices: 13.4 us -> 17.9 us  [exchange(): return lax.all_to_all(pieces, axes, split_axis=0, concat_axis=0, tiled=True)]
    ppermute x9, waiting for transfers between devices: 38.5 us -> 35.5 us  [swap(): return lax.ppermute(piece, axes, [(i, i ^ step) for i in range(4)])]
    concatenate x1 -> x0, other arithmetic: 1.64 us -> none  [local(): jnp.concatenate([band_coeffs, own], axis=0)]
  transfers between devices with their start and end apart: 11 -> 11, of which waited for: 5 -> 5; matrix products, arithmetic and copies ran while one was open for 4% -> 3% of each run, Pallas kernels for 13% -> 12%
where the time goes in v2:
time: 126 us
  waiting for transfers between devices  53.4 us (42%)
  starting transfers between devices  26.1 us (21%)
  Pallas kernels  23.5 us (19%)
  blocking collectives  17 us (13%)
  local copies, waits for them, and re-layouts  4.93 us (4%)
    ppermute x9, waiting for transfers between devices, swap(): return lax.ppermute(piece, axes, [(i, i ^ step) for i in range(4)])  35.5 us
    all_to_all x2, waiting for transfers between devices, exchange(): return lax.all_to_all(pieces, axes, split_axis=0, concat_axis=0, tiled=True)  17.9 us
    all_to_all x1, blocking collectives, exchange(): return lax.all_to_all(pieces, axes, split_axis=0, concat_axis=0, tiled=True)  17 us
    all_to_all x2, starting transfers between devices, exchange(): return lax.all_to_all(pieces, axes, split_axis=0, concat_axis=0, tiled=True)  14.4 us
    ppermute x9, starting transfers between devices, swap(): return lax.ppermute(piece, axes, [(i, i ^ step) for i in range(4)])  11.8 us
    pallas_call x1, Pallas kernels, local(): pl.pallas_call(series_kernel, out_shape=pltpu.HBM((1024, NP), jnp.bfloat1...  6.98 us
    pallas_call x1, Pallas kernels, local(): pl.pallas_call(self_energy_kernel, out_shape=jax.ShapeDtypeStruct((16, 8,...  6.04 us
    pallas_call x1, Pallas kernels, local(): copies_call(split_groups_kernel, [pltpu.HBM((4, 8, 8, NP), jnp.bfloat16)]...  3.09 us
  transfers between devices with their start and end apart: 11, of which 5 were waited for; matrix products, arithmetic and copies ran while one was open for 3% of the time, Pallas kernels for 12%

profile of v2, /device:TPU:1, one launch (start us, length us, event | category | flops | bytes accessed | tf_op | source)
XLA Modules:
  0.0 125.9 jit_solution(4130457010905949765)
XLA Ops:
  0.0 0.1 pad_add_fusion.place_ref
  0.1 2.7 %shard_map.64 = (bf16[4,56,896]{2,1,0:T(8,128)(2,1)S(1)}, bf16[4,56,896]{2,1,0:T(8,128)(2,1)}, bf16[4,56,896]{2,1,0:T(8,128)(2,1)}, bf16[4,56,896]{2,1,0:T(8,128)(2,1)}) custom-call(s32[2]{0:T(128)S(1)} %pad_add_fusion.place_ref, bf16[4,2,2,56,896]{4,3,2,1,0:T(8,128)(2,1)} %bitcast.28), custom_call_target="tpu_custom_call" | custom-call | tf_op jit(solution)/shard_map/pallas_call | solution.py:224
  2.7 1.5 %collective-permute-start = (bf16[4,56,896]{2,1,0:T(8,128)(2,1)}, bf16[4,56,896]{2,1,0:T(8,128)(2,1)S(1)}, u32[]{:S(2)}, u32[]{:S(2)}) collective-permute-start(bf16[4,56,896]{2,1,0:T(8,128)(2,1)} %get-tuple-element.23), channel_id=1, source_target_pairs={{0,8},{8,0},{16,24},{24,16},{1,9},{9,1},{17,25},{25,17},{2,10},{10... | collective-permute-start | bytes 1204232 | tf_op jit(solution)/shard_map/ppermute | solution.py:34
  4.2 1.7 %collective-permute-start.1 = (bf16[4,56,896]{2,1,0:T(8,128)(2,1)}, bf16[4,56,896]{2,1,0:T(8,128)(2,1)S(1)}, u32[]{:S(2)}, u32[]{:S(2)}) collective-permute-start(bf16[4,56,896]{2,1,0:T(8,128)(2,1)} %get-tuple-element.24), channel_id=1, source_target_pairs={{0,16},{8,24},{16,0},{24,8},{1,17},{9,25},{17,1},{25,9},{2,18},{10... | collective-permute-start | bytes 1204232 | tf_op jit(solution)/shard_map/ppermute | solution.py:34
  6.0 0.1 collective-permute-start.2
  6.0 2.9 %shard_map.66 = (bf16[8,4,8,896]{3,2,1,0:T(8,128)(2,1)}, bf16[8,4,8,896]{3,2,1,0:T(8,128)(2,1)}, bf16[8,4,8,896]{3,2,1,0:T(8,128)(2,1)}, bf16[8,4,8,896]{3,2,1,0:T(8,128)(2,1)}) custom-call(s32[2]{0:T(128)S(1)} %pad_add_fusion.place_ref, bf16[8,14,8,896]{3,2,1,0:T(8,128)(2,1)} %bitcast.30), custom_call_target="tpu_custom_call" | custom-call | flops 99999997952 | bytes 4194304 | tf_op jit(solution)/shard_map/pallas_call | solution.py:234
  8.9 1.4 %collective-permute-start.3 = (bf16[8,4,8,896]{3,2,1,0:T(8,128)(2,1)}, bf16[8,4,8,896]{3,2,1,0:T(8,128)(2,1)S(1)}, u32[]{:S(2)}, u32[]{:S(2)}) collective-permute-start(bf16[8,4,8,896]{3,2,1,0:T(8,128)(2,1)} %get-tuple-element.27), channel_id=1, source_target_pairs={{0,32},{32,0},{64,96},{96,64},{1,33},{33,1},{65,97},{97,65},{2,34}... | collective-permute-start | bytes 1376264 | tf_op jit(solution)/shard_map/ppermute | solution.py:34
  10.3 2.6 %collective-permute-start.4 = (bf16[8,4,8,896]{3,2,1,0:T(8,128)(2,1)}, bf16[8,4,8,896]{3,2,1,0:T(8,128)(2,1)S(1)}, u32[]{:S(2)}, u32[]{:S(2)}) collective-permute-start(bf16[8,4,8,896]{3,2,1,0:T(8,128)(2,1)} %get-tuple-element.28), channel_id=1, source_target_pairs={{0,64},{32,96},{64,0},{96,32},{1,65},{33,97},{65,1},{97,33},{2,66}... | collective-permute-start | bytes 1376264 | tf_op jit(solution)/shard_map/ppermute | solution.py:34
  12.9 0.7 constant_dynamic-slice_fusion.refs_5_
  13.6 0.8 dynamic-slice_bitcast_fusion.2.narrow_ref
  14.4 0.9 dynamic-slice_bitcast_fusion.1.wide_ref
  15.3 0.9 dynamic-slice_bitcast_fusion.table_ref
  16.2 0.0 collective-permute-done.first_ref
  16.2 0.1 collective-permute-start.5
  16.3 8.4 %collective-permute-done.2.third_ref = bf16[4,56,896]{2,1,0:T(8,128)(2,1)S(1)} collective-permute-done((bf16[4,56,896]{2,1,0:T(8,128)(2,1)}, bf16[4,56,896]{2,1,0:T(8,128)(2,1)S(1)}, u32[]{:S(2)}, u32[]{:S(2)}) %collective-permute-start.2) | collective-permute-done | bytes 401440 | tf_op jit(solution)/shard_map/ppermute | solution.py:34
  24.7 1.9 %shard_map.65 = bf16[16,56,896]{2,1,0:T(8,128)(2,1)} custom-call(bf16[4,56,896]{2,1,0:T(8,128)(2,1)S(1)} %get-tuple-element.22.own_ref, bf16[4,56,896]{2,1,0:T(8,128)(2,1)S(1)} %collective-permute-done.first_ref, bf16[4,56,896]{2,1,0:T(8,128)(2,1)S(1)} %collective-permute-done.1.second_ref, bf16[4,56,896]{2,1,0:T(8,128)(2,1)S(1)} %collective-permute-done.2.third_ref, ...), custom_call_target="tpu_custom_call" | custom-call | flops 99999997952 | bytes 4194304 | tf_op jit(solution)/shard_map/pallas_call | solution.py:244
  26.6 7.5 %all-to-all-start = ((bf16[16,56,896]{2,1,0:T(8,128)(2,1)}), bf16[16,56,896]{2,1,0:T(8,128)(2,1)S(1)}, u32[]{:S(2)}, u32[]{:S(2)}) async-start(bf16[16,56,896]{2,1,0:T(8,128)(2,1)} %shard_map.65), calls=%async_computation | async-start | bytes 3211264 | tf_op jit(solution)/shard_map/all_to_all | solution.py:30
  34.1 4.7 %collective-permute-done.5.refs_3_ = bf16[8,4,8,896]{3,2,1,0:T(8,128)(2,1)} collective-permute-done((bf16[8,4,8,896]{3,2,1,0:T(8,128)(2,1)}, bf16[8,4,8,896]{3,2,1,0:T(8,128)(2,1)}, u32[]{:S(2)}, u32[]{:S(2)}) %collective-permute-start.5) | collective-permute-done | bytes 458784 | tf_op jit(solution)/shard_map/ppermute | solution.py:34
  38.8 1.0 copy-done.3
  39.8 3.1 %shard_map.67 = (bf16[4,8,8,896]{3,2,1,0:T(8,128)(2,1)}, bf16[4,8,8,896]{3,2,1,0:T(8,128)(2,1)}, bf16[4,8,8,896]{3,2,1,0:T(8,128)(2,1)}, bf16[4,8,8,896]{3,2,1,0:T(8,128)(2,1)}) custom-call(s32[2]{0:T(128)S(1)} %pad_add_fusion.place_ref, bf16[8,4,8,896]{3,2,1,0:T(8,128)(2,1)S(1)} %copy-done.3, bf16[8,4,8,896]{3,2,1,0:T(8,128)(2,1)S(1)} %collective-permute-done.3.refs_1_, ...), custom_call_target="tpu_custom_call" | custom-call | flops 99999997952 | bytes 4194304 | tf_op jit(solution)/shard_map/pallas_call | solution.py:252
  42.9 15.1 %all-to-all-done = bf16[16,56,896]{2,1,0:T(8,128)(2,1)S(1)} async-done(((bf16[16,56,896]{2,1,0:T(8,128)(2,1)}), bf16[16,56,896]{2,1,0:T(8,128)(2,1)S(1)}, u32[]{:S(2)}, u32[]{:S(2)}) %all-to-all-start) | async-done | bytes 1605664 | tf_op jit(solution)/shard_map/all_to_all | solution.py:30
  58.0 0.4 collective-permute-start.7
  58.4 2.7 %collective-permute-start.8 = (bf16[4,8,8,896]{3,2,1,0:T(8,128)(2,1)}, bf16[4,8,8,896]{3,2,1,0:T(8,128)(2,1)S(1)}, u32[]{:S(2)}, u32[]{:S(2)}) collective-permute-start(bf16[4,8,8,896]{3,2,1,0:T(8,128)(2,1)} %get-tuple-element.38), channel_id=1, source_target_pairs={{0,24},{8,16},{16,8},{24,0},{1,25},{9,17},{17,9},{25,1},{2,26},{10... | collective-permute-start | bytes 1376264 | tf_op jit(solution)/shard_map/ppermute | solution.py:34
  61.1 7.0 %shard_map.68 = bf16[1024,896]{1,0:T(8,128)(2,1)} custom-call(bf16[896,896]{1,0:T(8,128)(2,1)S(1)} %bitcast.20), custom_call_target="tpu_custom_call" | custom-call | flops 99999997952 | bytes 4194304 | tf_op jit(solution)/shard_map/pallas_call | solution.py:273
  68.1 6.9 %all-to-all-start.1 = ((bf16[128,8,896]{2,1,0:T(8,128)(2,1)}), bf16[128,8,896]{2,1,0:T(8,128)(2,1)S(1)}, u32[]{:S(2)}, u32[]{:S(2)}) async-start(bf16[128,8,896]{2,1,0:T(8,128)(2,1)} %bitcast.27), calls=%async_computation.1 | async-start | bytes 3670016 | tf_op jit(solution)/shard_map/all_to_all | solution.py:30
  75.0 1.3 %collective-permute-start.6 = (bf16[4,8,8,896]{3,2,1,0:T(8,128)(2,1)}, bf16[4,8,8,896]{3,2,1,0:T(8,128)(2,1)S(1)}, u32[]{:S(2)}, u32[]{:S(2)}) collective-permute-start(bf16[4,8,8,896]{3,2,1,0:T(8,128)(2,1)} %get-tuple-element.36), channel_id=1, source_target_pairs={{0,8},{8,0},{16,24},{24,16},{1,9},{9,1},{17,25},{25,17},{2,10},{10... | collective-permute-start | bytes 1376264 | tf_op jit(solution)/shard_map/ppermute | solution.py:34
  76.3 22.4 %collective-permute-done.8 = bf16[4,8,8,896]{3,2,1,0:T(8,128)(2,1)S(1)} collective-permute-done((bf16[4,8,8,896]{3,2,1,0:T(8,128)(2,1)}, bf16[4,8,8,896]{3,2,1,0:T(8,128)(2,1)S(1)}, u32[]{:S(2)}, u32[]{:S(2)}) %collective-permute-start.8) | collective-permute-done | bytes 458784 | tf_op jit(solution)/shard_map/ppermute | solution.py:34
  98.7 0.6 copy-done
  99.3 2.8 %all-to-all-done.1 = bf16[128,8,896]{2,1,0:T(8,128)(2,1)S(1)} async-done(((bf16[128,8,896]{2,1,0:T(8,128)(2,1)}), bf16[128,8,896]{2,1,0:T(8,128)(2,1)S(1)}, u32[]{:S(2)}, u32[]{:S(2)}) %all-to-all-start.1) | async-done | bytes 1835040 | tf_op jit(solution)/shard_map/all_to_all | solution.py:30
  102.1 6.0 %shard_map.70 = bf16[16,8,8,128]{3,2,1,0:T(8,128)(2,1)S(1)} custom-call(s32[2]{0:T(128)S(1)} %copy-done.2, bf16[1024,896]{1,0:T(8,128)(2,1)S(1)} %bitcast.19, bf16[256,256]{1,0:T(8,128)(2,1)S(1)} %dynamic-slice_bitcast_fusion.table_ref, bf16[4,64,896]{2,1,0:T(8,128)(2,1)} %bitcast.29, bf16[4,64,896]{2,1,0:T(8,128)(2,1)S(1)} %bitcast.26, ...), custom_call_target="tpu_custom_call" | custom-call | tf_op jit(solution)/shard_map/pallas_call | solution.py:287
  108.2 17.0 %all_to_all.15 = bf16[128,8,128]{2,1,0:T(8,128)(2,1)S(1)} all-to-all(bf16[128,8,128]{2,1,0:T(8,128)(2,1)S(1)} %bitcast.21), channel_id=1, replica_groups=mesh['mom'=4,'zlo'=2,'core'=2,'x'=4,'zhi'=2] {'mom','zlo','core','x','zhi'}, dimensions={0} | all-to-all | bytes 524288 | tf_op jit(solution)/shard_map/all_to_all | solution.py:30
  125.2 0.7 convert_reduce_fusion
  (12 shorter events, 0.0 us)
Async XLA Ops:
  0.1 38.7 %copy-start.1 = (s32[2]{0:T(128)}, s32[2]{0:T(128)S(1)}, u32[]{:S(2)}) copy-start(s32[2]{0:T(128)S(1)} %pad_add_fusion.place_ref) | copy-start | bytes 28
  2.7 13.5 %collective-permute-start = (bf16[4,56,896]{2,1,0:T(8,128)(2,1)}, bf16[4,56,896]{2,1,0:T(8,128)(2,1)S(1)}, u32[]{:S(2)}, u32[]{:S(2)}) collective-permute-start(bf16[4,56,896]{2,1,0:T(8,128)(2,1)} %get-tuple-element.23), channel_id=1, source_target_pairs={{0,8},{8,0},{16,24},{24,16},{1,9},{9,1},{17,25},{25,17},{2,10},{10... | collective-permute-start | bytes 1204232 | tf_op jit(solution)/shard_map/ppermute | solution.py:34
  4.2 12.1 %collective-permute-start.1 = (bf16[4,56,896]{2,1,0:T(8,128)(2,1)}, bf16[4,56,896]{2,1,0:T(8,128)(2,1)S(1)}, u32[]{:S(2)}, u32[]{:S(2)}) collective-permute-start(bf16[4,56,896]{2,1,0:T(8,128)(2,1)} %get-tuple-element.24), channel_id=1, source_target_pairs={{0,16},{8,24},{16,0},{24,8},{1,17},{9,25},{17,1},{25,9},{2,18},{10... | collective-permute-start | bytes 1204232 | tf_op jit(solution)/shard_map/ppermute | solution.py:34
  6.0 18.8 %collective-permute-start.2 = (bf16[4,56,896]{2,1,0:T(8,128)(2,1)}, bf16[4,56,896]{2,1,0:T(8,128)(2,1)S(1)}, u32[]{:S(2)}, u32[]{:S(2)}) collective-permute-start(bf16[4,56,896]{2,1,0:T(8,128)(2,1)} %get-tuple-element.25), channel_id=1, source_target_pairs={{0,24},{8,16},{16,8},{24,0},{1,25},{9,17},{17,9},{25,1},{2,26},{10... | collective-permute-start | bytes 1204232 | tf_op jit(solution)/shard_map/ppermute | solution.py:34
  8.9 25.2 %collective-permute-start.3 = (bf16[8,4,8,896]{3,2,1,0:T(8,128)(2,1)}, bf16[8,4,8,896]{3,2,1,0:T(8,128)(2,1)S(1)}, u32[]{:S(2)}, u32[]{:S(2)}) collective-permute-start(bf16[8,4,8,896]{3,2,1,0:T(8,128)(2,1)} %get-tuple-element.27), channel_id=1, source_target_pairs={{0,32},{32,0},{64,96},{96,64},{1,33},{33,1},{65,97},{97,65},{2,34}... | collective-permute-start | bytes 1376264 | tf_op jit(solution)/shard_map/ppermute | solution.py:34
  10.3 23.8 %collective-permute-start.4 = (bf16[8,4,8,896]{3,2,1,0:T(8,128)(2,1)}, bf16[8,4,8,896]{3,2,1,0:T(8,128)(2,1)S(1)}, u32[]{:S(2)}, u32[]{:S(2)}) collective-permute-start(bf16[8,4,8,896]{3,2,1,0:T(8,128)(2,1)} %get-tuple-element.28), channel_id=1, source_target_pairs={{0,64},{32,96},{64,0},{96,32},{1,65},{33,97},{65,1},{97,33},{2,66}... | collective-permute-start | bytes 1376264 | tf_op jit(solution)/shard_map/ppermute | solution.py:34
  16.2 22.6 %collective-permute-start.5 = (bf16[8,4,8,896]{3,2,1,0:T(8,128)(2,1)}, bf16[8,4,8,896]{3,2,1,0:T(8,128)(2,1)}, u32[]{:S(2)}, u32[]{:S(2)}) collective-permute-start(bf16[8,4,8,896]{3,2,1,0:T(8,128)(2,1)} %get-tuple-element.29), channel_id=1, source_target_pairs={{0,96},{32,64},{64,32},{96,0},{1,97},{33,65},{65,33},{97,1},{2,98}... | collective-permute-start | bytes 1376264 | tf_op jit(solution)/shard_map/ppermute | solution.py:34
  26.6 31.4 %all-to-all-start = ((bf16[16,56,896]{2,1,0:T(8,128)(2,1)}), bf16[16,56,896]{2,1,0:T(8,128)(2,1)S(1)}, u32[]{:S(2)}, u32[]{:S(2)}) async-start(bf16[16,56,896]{2,1,0:T(8,128)(2,1)} %shard_map.65), calls=%async_computation | async-start | bytes 3211264 | tf_op jit(solution)/shard_map/all_to_all | solution.py:30
  38.8 1.0 copy-start.3
  58.0 18.3 %collective-permute-start.7 = (bf16[4,8,8,896]{3,2,1,0:T(8,128)(2,1)}, bf16[4,8,8,896]{3,2,1,0:T(8,128)(2,1)S(1)}, u32[]{:S(2)}, u32[]{:S(2)}) collective-permute-start(bf16[4,8,8,896]{3,2,1,0:T(8,128)(2,1)} %get-tuple-element.37), channel_id=1, source_target_pairs={{0,16},{8,24},{16,0},{24,8},{1,17},{9,25},{17,1},{25,9},{2,18},{10... | collective-permute-start | bytes 1376264 | tf_op jit(solution)/shard_map/ppermute | solution.py:34
  58.4 40.3 %collective-permute-start.8 = (bf16[4,8,8,896]{3,2,1,0:T(8,128)(2,1)}, bf16[4,8,8,896]{3,2,1,0:T(8,128)(2,1)S(1)}, u32[]{:S(2)}, u32[]{:S(2)}) collective-permute-start(bf16[4,8,8,896]{3,2,1,0:T(8,128)(2,1)} %get-tuple-element.38), channel_id=1, source_target_pairs={{0,24},{8,16},{16,8},{24,0},{1,25},{9,17},{17,9},{25,1},{2,26},{10... | collective-permute-start | bytes 1376264 | tf_op jit(solution)/shard_map/ppermute | solution.py:34
  68.1 34.1 %all-to-all-start.1 = ((bf16[128,8,896]{2,1,0:T(8,128)(2,1)}), bf16[128,8,896]{2,1,0:T(8,128)(2,1)S(1)}, u32[]{:S(2)}, u32[]{:S(2)}) async-start(bf16[128,8,896]{2,1,0:T(8,128)(2,1)} %bitcast.27), calls=%async_computation.1 | async-start | bytes 3670016 | tf_op jit(solution)/shard_map/all_to_all | solution.py:30
  75.0 24.3 %collective-permute-start.6 = (bf16[4,8,8,896]{3,2,1,0:T(8,128)(2,1)}, bf16[4,8,8,896]{3,2,1,0:T(8,128)(2,1)S(1)}, u32[]{:S(2)}, u32[]{:S(2)}) collective-permute-start(bf16[4,8,8,896]{3,2,1,0:T(8,128)(2,1)} %get-tuple-element.36), channel_id=1, source_target_pairs={{0,8},{8,0},{16,24},{24,16},{1,9},{9,1},{17,25},{25,17},{2,10},{10... | collective-permute-start | bytes 1376264 | tf_op jit(solution)/shard_map/ppermute | solution.py:34
  98.7 3.4 %copy-start.2 = (s32[2]{0:T(128)S(1)}, s32[2]{0:T(128)}, u32[]{:S(2)}) copy-start(s32[2]{0:T(128)} %copy-done.1) | copy-start | bytes 28
  98.7 0.6 copy-start

commit v3 on v2

--- a/solution.py
+++ b/solution.py
@@ -52,11 +52,14 @@
     rows = jnp.concatenate([piece[t, 48:56, :].astype(jnp.float32) for piece in pieces for t in range(4)], axis=0)
     mixed = jnp.dot(narrow_ref[...], rows.astype(jnp.bfloat16), preferred_element_type=jnp.float32) * scale
     mixed_ref[:, 48:56, :] = mixed.reshape(NT, 8, NP).astype(jnp.bfloat16)
+    moves = start_all([(mixed_ref.at[:, pl.ds(48, 8)], out_ref.at[:, pl.ds(48, 8)])], sent.at[pl.ds(0, 1)])
     for at in range(0, 48, 16):
         rows = jnp.concatenate([piece[t, at : at + 16, :] for piece in pieces for t in range(4)], axis=0)
         mixed = jnp.dot(wide_ref[...], rows, preferred_element_type=jnp.float32) * scale
         mixed_ref[:, at : at + 16, :] = mixed.reshape(NT, 16, NP).astype(jnp.bfloat16)
-    copy_all([(mixed_ref.at[pl.ds(4 * i, 4)], out_ref.at[pl.ds(4 * i, 4)]) for i in range(4)], sent)
+        moves += start_all([(mixed_ref.at[:, pl.ds(at, 16)], out_ref.at[:, pl.ds(at, 16)])], sent.at[pl.ds(1 + at // 16, 1)])
+    for move in moves:
+        move.wait()
 
 
 def series_kernel(tile_ref, out_ref, square_ref, sum_ref, fourth_ref, left_ref, right_ref, padded_ref, sent):
@@ -127,11 +130,22 @@
             for move in moves[:2]:
                 move.wait()
         applied = jnp.dot(sigma_ref[step], coeffs_ref[...], preferred_element_type=jnp.float32)
-        values = jnp.sum(applied.reshape(32, 8, NB) * own[None], axis=1)
+        values = row_sums(applied.reshape(32, 8, NB) * own[None])
         for mom in range(4):
             for p in range(8):
                 share = values[8 * mom : 8 * mom + 8, 128 * p : 128 * p + 128]
                 out_ref[4 * mom + (tm_here ^ step), p] = share.astype(out_ref.dtype)
+
+
+def row_sums(x):
+    n = x.shape[-1]
+    x = x.reshape(4, 8, 8, n)
+    row = lax.broadcasted_iota(jnp.int32, (1, 1, 8, n), 2)
+    turn = lambda v, by: pltpu.roll(v.reshape(-1, 8, n), by, 1).reshape(v.shape)
+    for half in (4, 2, 1):
+        low, high = x[:, :half], x[:, half:]
+        x = jnp.where(row % (2 * half) < half, low + turn(low, 8 - half), high + turn(high, half))
+    return x.reshape(32, n)
 
 
 def start_all(copies, done):
@@ -229,8 +243,9 @@
         scratch_shapes=[pltpu.VMEM((3, *quarter), jnp.bfloat16), sems(4), sems(4)],
         compiler_params=vmem(4),
     )(place, in_hbm(chi_time.reshape(4, 2, 2, 56, NP)))
-    received = [pieces[0]] + [swap(pieces[step], TM, step) for step in (1, 2, 3)]
-
+    pieces = list(pieces)
+
+    green, pieces[1] = lax.optimization_barrier((green, pieces[1]))
     parts = copies_call(
         split_rows_kernel,
         [pltpu.HBM((8, 4, 8, NP), jnp.bfloat16)] * 4,
@@ -239,6 +254,7 @@
         [pltpu.VMEM((4, 8, 4, 8, NP), jnp.bfloat16), sems(4), sems(4)],
         cost=long,
     )(place, in_hbm(green.reshape(8, GROUPS, 8, NP)))
+    received = [pieces[0]] + [swap(pieces[step], TM, step) for step in (1, 2, 3)]
     by_mom = [parts[0]] + [swap(parts[step], "mom", step) for step in (1, 2, 3)]
 
     mixed = pl.pallas_call(
@@ -258,7 +274,6 @@
         cost=long,
     )(place, *by_mom)
     tile = exchange(mixed, PLANE).reshape(NP, NP)
-    tile, groups = lax.optimization_barrier((tile, groups))
     cells = [groups[0]] + [swap(groups[step], TM, step) for step in (1, 2, 3)]
     cells = [cell.reshape(4, 64, NP) for cell in cells]
     arrived = pl.pallas_call(
@@ -277,7 +292,7 @@
         scratch_shapes=[square, square, pltpu.VMEM((NP, NP), jnp.float32), square, square]
         + [pltpu.VMEM((1024, NP), jnp.bfloat16), sems(5)],
         compiler_params=vmem(16),
-        cost_estimate=long,
+        cost_estimate=None,
     )(tile)
     spread = exchange(screened.reshape(128, 8, NP), BY_ROWS).reshape(1024, NP)
 

time: 126 us -> 122 us (0.968)
  Pallas kernels: 23.5 us -> 21.7 us
  waiting for transfers between devices: 53.4 us -> 51.7 us
  blocking collectives: 17 us -> 15.6 us
    ppermute x9, waiting for transfers between devices: 35.5 us -> 14.1 us  [swap(): return lax.ppermute(piece, axes, [(i, i ^ step) for i in range(4)])]
    all_to_all x2, waiting for transfers between devices: 17.9 us -> 37.7 us  [exchange(): return lax.all_to_all(pieces, axes, split_axis=0, concat_axis=0, tiled=True)]
    all_to_all x1, blocking collectives: 17 us -> 15.6 us  [exchange(): return lax.all_to_all(pieces, axes, split_axis=0, concat_axis=0, tiled=True)]
  transfers between devices with their start and end apart: 11 -> 11, of which waited for: 5 -> 6; matrix products, arithmetic and copies ran while one was open for 3% -> 3% of each run, Pallas kernels for 12% -> 11%
where the time goes in v3:
time: 122 us
  waiting for transfers between devices  51.7 us (42%)
  starting transfers between devices  26.6 us (22%)
  Pallas kernels  21.7 us (18%)
  blocking collectives  15.6 us (13%)
  local copies, waits for them, and re-layouts  4.91 us (4%)
    all_to_all x2, waiting for transfers between devices, exchange(): return lax.all_to_all(pieces, axes, split_axis=0, concat_axis=0, tiled=True)  37.7 us
    all_to_all x1, blocking collectives, exchange(): return lax.all_to_all(pieces, axes, split_axis=0, concat_axis=0, tiled=True)  15.6 us
    all_to_all x2, starting transfers between devices, exchange(): return lax.all_to_all(pieces, axes, split_axis=0, concat_axis=0, tiled=True)  15.3 us
    ppermute x9, waiting for transfers between devices, swap(): return lax.ppermute(piece, axes, [(i, i ^ step) for i in range(4)])  14.1 us
    ppermute x9, starting transfers between devices, swap(): return lax.ppermute(piece, axes, [(i, i ^ step) for i in range(4)])  11.3 us
    pallas_call x1, Pallas kernels, local(): pl.pallas_call(series_kernel, out_shape=pltpu.HBM((1024, NP), jnp.bfloat1...  7 us
    pallas_call x1, Pallas kernels, local(): pl.pallas_call(self_energy_kernel, out_shape=jax.ShapeDtypeStruct((16, 8,...  5.39 us
    pallas_call x1, Pallas kernels, local(): copies_call(split_rows_kernel, [pltpu.HBM((8, 4, 8, NP), jnp.bfloat16)] *...  2.85 us
  transfers between devices with their start and end apart: 11, of which 6 were waited for; matrix products, arithmetic and copies ran while one was open for 3% of the time, Pallas kernels for 11%

profile of v3, /device:TPU:1, one launch (start us, length us, event | category | flops | bytes accessed | tf_op | source)
XLA Modules:
  0.0 121.5 jit_solution(11688906468312168488)
XLA Ops:
  0.0 0.1 pad_add_fusion.place_ref
  0.1 2.7 %shard_map.64 = (bf16[4,56,896]{2,1,0:T(8,128)(2,1)S(1)}, bf16[4,56,896]{2,1,0:T(8,128)(2,1)}, bf16[4,56,896]{2,1,0:T(8,128)(2,1)}, bf16[4,56,896]{2,1,0:T(8,128)(2,1)}) custom-call(s32[2]{0:T(128)S(1)} %pad_add_fusion.place_ref, bf16[4,2,2,56,896]{4,3,2,1,0:T(8,128)(2,1)} %bitcast.28), custom_call_target="tpu_custom_call" | custom-call | tf_op jit(solution)/shard_map/pallas_call | solution.py:238
  2.8 1.5 %collective-permute-start = (bf16[4,56,896]{2,1,0:T(8,128)(2,1)}, bf16[4,56,896]{2,1,0:T(8,128)(2,1)S(1)}, u32[]{:S(2)}, u32[]{:S(2)}) collective-permute-start(bf16[4,56,896]{2,1,0:T(8,128)(2,1)} %get-tuple-element.21), channel_id=1, source_target_pairs={{0,8},{8,0},{16,24},{24,16},{1,9},{9,1},{17,25},{25,17},{2,10},{10... | collective-permute-start | bytes 1204232 | tf_op jit(solution)/shard_map/ppermute | solution.py:34
  4.3 1.7 %collective-permute-start.1 = (bf16[4,56,896]{2,1,0:T(8,128)(2,1)}, bf16[4,56,896]{2,1,0:T(8,128)(2,1)S(1)}, u32[]{:S(2)}, u32[]{:S(2)}) collective-permute-start(bf16[4,56,896]{2,1,0:T(8,128)(2,1)} %get-tuple-element.22), channel_id=1, source_target_pairs={{0,16},{8,24},{16,0},{24,8},{1,17},{9,25},{17,1},{25,9},{2,18},{10... | collective-permute-start | bytes 1204232 | tf_op jit(solution)/shard_map/ppermute | solution.py:34
  6.0 0.1 collective-permute-start.2
  6.1 2.9 %shard_map.67 = (bf16[8,4,8,896]{3,2,1,0:T(8,128)(2,1)}, bf16[8,4,8,896]{3,2,1,0:T(8,128)(2,1)}, bf16[8,4,8,896]{3,2,1,0:T(8,128)(2,1)}, bf16[8,4,8,896]{3,2,1,0:T(8,128)(2,1)}) custom-call(s32[2]{0:T(128)S(1)} %pad_add_fusion.place_ref, bf16[8,14,8,896]{3,2,1,0:T(8,128)(2,1)} %bitcast.30), custom_call_target="tpu_custom_call" | custom-call | flops 99999997952 | bytes 4194304 | tf_op jit(solution)/shard_map/pallas_call | solution.py:249
  8.9 1.4 %collective-permute-start.3 = (bf16[8,4,8,896]{3,2,1,0:T(8,128)(2,1)}, bf16[8,4,8,896]{3,2,1,0:T(8,128)(2,1)S(1)}, u32[]{:S(2)}, u32[]{:S(2)}) collective-permute-start(bf16[8,4,8,896]{3,2,1,0:T(8,128)(2,1)} %get-tuple-element.26), channel_id=1, source_target_pairs={{0,32},{32,0},{64,96},{96,64},{1,33},{33,1},{65,97},{97,65},{2,34}... | collective-permute-start | bytes 1376264 | tf_op jit(solution)/shard_map/ppermute | solution.py:34
  10.3 2.6 %collective-permute-start.4 = (bf16[8,4,8,896]{3,2,1,0:T(8,128)(2,1)}, bf16[8,4,8,896]{3,2,1,0:T(8,128)(2,1)S(1)}, u32[]{:S(2)}, u32[]{:S(2)}) collective-permute-start(bf16[8,4,8,896]{3,2,1,0:T(8,128)(2,1)} %get-tuple-element.27), channel_id=1, source_target_pairs={{0,64},{32,96},{64,0},{96,32},{1,65},{33,97},{65,1},{97,33},{2,66}... | collective-permute-start | bytes 1376264 | tf_op jit(solution)/shard_map/ppermute | solution.py:34
  12.9 0.8 dynamic-slice_bitcast_fusion.2.narrow_ref
  13.7 0.9 dynamic-slice_bitcast_fusion.1.wide_ref
  14.6 0.1 collective-permute-start.5
  14.7 1.0 collective-permute-done.1.second_ref
  15.8 8.9 %collective-permute-done.2.third_ref = bf16[4,56,896]{2,1,0:T(8,128)(2,1)S(1)} collective-permute-done((bf16[4,56,896]{2,1,0:T(8,128)(2,1)}, bf16[4,56,896]{2,1,0:T(8,128)(2,1)S(1)}, u32[]{:S(2)}, u32[]{:S(2)}) %collective-permute-start.2) | collective-permute-done | bytes 401440 | tf_op jit(solution)/shard_map/ppermute | solution.py:34
  24.7 1.5 %shard_map.65 = bf16[16,56,896]{2,1,0:T(8,128)(2,1)} custom-call(bf16[4,56,896]{2,1,0:T(8,128)(2,1)S(1)} %get-tuple-element.19.own_ref, bf16[4,56,896]{2,1,0:T(8,128)(2,1)S(1)} %collective-permute-done.first_ref, bf16[4,56,896]{2,1,0:T(8,128)(2,1)S(1)} %collective-permute-done.1.second_ref, bf16[4,56,896]{2,1,0:T(8,128)(2,1)S(1)} %collective-permute-done.2.third_ref, ...), custom_call_target="tpu_custom_call" | custom-call | flops 99999997952 | bytes 4194304 | tf_op jit(solution)/shard_map/pallas_call | solution.py:260
  26.2 7.5 %all-to-all-start = ((bf16[16,56,896]{2,1,0:T(8,128)(2,1)}), bf16[16,56,896]{2,1,0:T(8,128)(2,1)S(1)}, u32[]{:S(2)}, u32[]{:S(2)}) async-start(bf16[16,56,896]{2,1,0:T(8,128)(2,1)} %shard_map.65), calls=%async_computation | async-start | bytes 3211264 | tf_op jit(solution)/shard_map/all_to_all | solution.py:30
  33.7 3.4 %collective-permute-done.5.refs_3_ = bf16[8,4,8,896]{3,2,1,0:T(8,128)(2,1)S(1)} collective-permute-done((bf16[8,4,8,896]{3,2,1,0:T(8,128)(2,1)}, bf16[8,4,8,896]{3,2,1,0:T(8,128)(2,1)S(1)}, u32[]{:S(2)}, u32[]{:S(2)}) %collective-permute-start.5) | collective-permute-done | bytes 458784 | tf_op jit(solution)/shard_map/ppermute | solution.py:34
  37.1 1.0 copy-done.1
  38.1 2.3 %shard_map.68 = (bf16[4,8,8,896]{3,2,1,0:T(8,128)(2,1)}, bf16[4,8,8,896]{3,2,1,0:T(8,128)(2,1)}, bf16[4,8,8,896]{3,2,1,0:T(8,128)(2,1)}, bf16[4,8,8,896]{3,2,1,0:T(8,128)(2,1)}) custom-call(s32[2]{0:T(128)S(1)} %pad_add_fusion.place_ref, bf16[8,4,8,896]{3,2,1,0:T(8,128)(2,1)S(1)} %copy-done.1, bf16[8,4,8,896]{3,2,1,0:T(8,128)(2,1)S(1)} %collective-permute-done.3.refs_1_, ...), custom_call_target="tpu_custom_call" | custom-call | flops 99999997952 | bytes 4194304 | tf_op jit(solution)/shard_map/pallas_call | solution.py:268
  40.4 1.9 %collective-permute-start.7 = (bf16[4,8,8,896]{3,2,1,0:T(8,128)(2,1)}, bf16[4,8,8,896]{3,2,1,0:T(8,128)(2,1)S(1)}, u32[]{:S(2)}, u32[]{:S(2)}) collective-permute-start(bf16[4,8,8,896]{3,2,1,0:T(8,128)(2,1)} %get-tuple-element.31), channel_id=1, source_target_pairs={{0,16},{8,24},{16,0},{24,8},{1,17},{9,25},{17,1},{25,9},{2,18},{10... | collective-permute-start | bytes 1376264 | tf_op jit(solution)/shard_map/ppermute | solution.py:34
  42.3 1.6 %collective-permute-start.8 = (bf16[4,8,8,896]{3,2,1,0:T(8,128)(2,1)}, bf16[4,8,8,896]{3,2,1,0:T(8,128)(2,1)S(1)}, u32[]{:S(2)}, u32[]{:S(2)}) collective-permute-start(bf16[4,8,8,896]{3,2,1,0:T(8,128)(2,1)} %get-tuple-element.32), channel_id=1, source_target_pairs={{0,24},{8,16},{16,8},{24,0},{1,25},{9,17},{17,9},{25,1},{2,26},{10... | collective-permute-start | bytes 1376264 | tf_op jit(solution)/shard_map/ppermute | solution.py:34
  43.9 0.7 constant_dynamic-slice_fusion.refs_5_
  44.6 0.9 dynamic-slice_bitcast_fusion.table_ref
  45.5 0.4 collective-permute-start.6
  45.9 11.8 %all-to-all-done = bf16[16,56,896]{2,1,0:T(8,128)(2,1)S(1)} async-done(((bf16[16,56,896]{2,1,0:T(8,128)(2,1)}), bf16[16,56,896]{2,1,0:T(8,128)(2,1)S(1)}, u32[]{:S(2)}, u32[]{:S(2)}) %all-to-all-start) | async-done | bytes 1605664 | tf_op jit(solution)/shard_map/all_to_all | solution.py:30
  57.7 7.0 %shard_map.66 = bf16[1024,896]{1,0:T(8,128)(2,1)} custom-call(bf16[896,896]{1,0:T(8,128)(2,1)S(1)} %bitcast.20), custom_call_target="tpu_custom_call" | custom-call | tf_op jit(solution)/shard_map/pallas_call | solution.py:288
  64.8 7.9 %all-to-all-start.1 = ((bf16[128,8,896]{2,1,0:T(8,128)(2,1)}), bf16[128,8,896]{2,1,0:T(8,128)(2,1)S(1)}, u32[]{:S(2)}, u32[]{:S(2)}) async-start(bf16[128,8,896]{2,1,0:T(8,128)(2,1)} %bitcast.27), calls=%async_computation.1 | async-start | bytes 3670016 | tf_op jit(solution)/shard_map/all_to_all | solution.py:30
  72.6 0.7 collective-permute-done.8
  73.3 0.6 copy-done
  73.9 25.8 %all-to-all-done.1 = bf16[128,8,896]{2,1,0:T(8,128)(2,1)S(1)} async-done(((bf16[128,8,896]{2,1,0:T(8,128)(2,1)}), bf16[128,8,896]{2,1,0:T(8,128)(2,1)S(1)}, u32[]{:S(2)}, u32[]{:S(2)}) %all-to-all-start.1) | async-done | bytes 1835040 | tf_op jit(solution)/shard_map/all_to_all | solution.py:30
  99.8 5.4 %shard_map.70 = bf16[16,8,8,128]{3,2,1,0:T(8,128)(2,1)S(1)} custom-call(s32[2]{0:T(128)S(1)} %pad_add_fusion.place_ref, bf16[1024,896]{1,0:T(8,128)(2,1)S(1)} %bitcast.19, bf16[256,256]{1,0:T(8,128)(2,1)S(1)} %dynamic-slice_bitcast_fusion.table_ref, bf16[4,64,896]{2,1,0:T(8,128)(2,1)} %bitcast.29, bf16[4,64,896]{2,1,0:T(8,128)(2,1)S(1)} %bitcast.26, ...), custom_call_target="tpu_custom_call" | custom-call | tf_op jit(solution)/shard_map/pallas_call | solution.py:302
  105.2 15.6 %all_to_all.15 = bf16[128,8,128]{2,1,0:T(8,128)(2,1)S(1)} all-to-all(bf16[128,8,128]{2,1,0:T(8,128)(2,1)S(1)} %bitcast.21), channel_id=1, replica_groups=mesh['mom'=4,'zlo'=2,'core'=2,'x'=4,'zhi'=2] {'mom','zlo','core','x','zhi'}, dimensions={0} | all-to-all | bytes 524288 | tf_op jit(solution)/shard_map/all_to_all | solution.py:30
  120.8 0.7 convert_reduce_fusion
  (8 shorter events, 0.0 us)
Async XLA Ops:
  2.8 11.8 %collective-permute-start = (bf16[4,56,896]{2,1,0:T(8,128)(2,1)}, bf16[4,56,896]{2,1,0:T(8,128)(2,1)S(1)}, u32[]{:S(2)}, u32[]{:S(2)}) collective-permute-start(bf16[4,56,896]{2,1,0:T(8,128)(2,1)} %get-tuple-element.21), channel_id=1, source_target_pairs={{0,8},{8,0},{16,24},{24,16},{1,9},{9,1},{17,25},{25,17},{2,10},{10... | collective-permute-start | bytes 1204232 | tf_op jit(solution)/shard_map/ppermute | solution.py:34
  4.3 11.5 %collective-permute-start.1 = (bf16[4,56,896]{2,1,0:T(8,128)(2,1)}, bf16[4,56,896]{2,1,0:T(8,128)(2,1)S(1)}, u32[]{:S(2)}, u32[]{:S(2)}) collective-permute-start(bf16[4,56,896]{2,1,0:T(8,128)(2,1)} %get-tuple-element.22), channel_id=1, source_target_pairs={{0,16},{8,24},{16,0},{24,8},{1,17},{9,25},{17,1},{25,9},{2,18},{10... | collective-permute-start | bytes 1204232 | tf_op jit(solution)/shard_map/ppermute | solution.py:34
  6.0 18.6 %collective-permute-start.2 = (bf16[4,56,896]{2,1,0:T(8,128)(2,1)}, bf16[4,56,896]{2,1,0:T(8,128)(2,1)S(1)}, u32[]{:S(2)}, u32[]{:S(2)}) collective-permute-start(bf16[4,56,896]{2,1,0:T(8,128)(2,1)} %get-tuple-element.23), channel_id=1, source_target_pairs={{0,24},{8,16},{16,8},{24,0},{1,25},{9,17},{17,9},{25,1},{2,26},{10... | collective-permute-start | bytes 1204232 | tf_op jit(solution)/shard_map/ppermute | solution.py:34
  8.9 24.7 %collective-permute-start.3 = (bf16[8,4,8,896]{3,2,1,0:T(8,128)(2,1)}, bf16[8,4,8,896]{3,2,1,0:T(8,128)(2,1)S(1)}, u32[]{:S(2)}, u32[]{:S(2)}) collective-permute-start(bf16[8,4,8,896]{3,2,1,0:T(8,128)(2,1)} %get-tuple-element.26), channel_id=1, source_target_pairs={{0,32},{32,0},{64,96},{96,64},{1,33},{33,1},{65,97},{97,65},{2,34}... | collective-permute-start | bytes 1376264 | tf_op jit(solution)/shard_map/ppermute | solution.py:34
  10.3 23.3 %collective-permute-start.4 = (bf16[8,4,8,896]{3,2,1,0:T(8,128)(2,1)}, bf16[8,4,8,896]{3,2,1,0:T(8,128)(2,1)S(1)}, u32[]{:S(2)}, u32[]{:S(2)}) collective-permute-start(bf16[8,4,8,896]{3,2,1,0:T(8,128)(2,1)} %get-tuple-element.27), channel_id=1, source_target_pairs={{0,64},{32,96},{64,0},{96,32},{1,65},{33,97},{65,1},{97,33},{2,66}... | collective-permute-start | bytes 1376264 | tf_op jit(solution)/shard_map/ppermute | solution.py:34
  14.6 22.5 %collective-permute-start.5 = (bf16[8,4,8,896]{3,2,1,0:T(8,128)(2,1)}, bf16[8,4,8,896]{3,2,1,0:T(8,128)(2,1)S(1)}, u32[]{:S(2)}, u32[]{:S(2)}) collective-permute-start(bf16[8,4,8,896]{3,2,1,0:T(8,128)(2,1)} %get-tuple-element.28), channel_id=1, source_target_pairs={{0,96},{32,64},{64,32},{96,0},{1,97},{33,65},{65,33},{97,1},{2,98}... | collective-permute-start | bytes 1376264 | tf_op jit(solution)/shard_map/ppermute | solution.py:34
  26.2 31.6 %all-to-all-start = ((bf16[16,56,896]{2,1,0:T(8,128)(2,1)}), bf16[16,56,896]{2,1,0:T(8,128)(2,1)S(1)}, u32[]{:S(2)}, u32[]{:S(2)}) async-start(bf16[16,56,896]{2,1,0:T(8,128)(2,1)} %shard_map.65), calls=%async_computation | async-start | bytes 3211264 | tf_op jit(solution)/shard_map/all_to_all | solution.py:30
  37.1 1.0 copy-start.1
  40.4 32.3 %collective-permute-start.7 = (bf16[4,8,8,896]{3,2,1,0:T(8,128)(2,1)}, bf16[4,8,8,896]{3,2,1,0:T(8,128)(2,1)S(1)}, u32[]{:S(2)}, u32[]{:S(2)}) collective-permute-start(bf16[4,8,8,896]{3,2,1,0:T(8,128)(2,1)} %get-tuple-element.31), channel_id=1, source_target_pairs={{0,16},{8,24},{16,0},{24,8},{1,17},{9,25},{17,1},{25,9},{2,18},{10... | collective-permute-start | bytes 1376264 | tf_op jit(solution)/shard_map/ppermute | solution.py:34
  42.3 31.0 %collective-permute-start.8 = (bf16[4,8,8,896]{3,2,1,0:T(8,128)(2,1)}, bf16[4,8,8,896]{3,2,1,0:T(8,128)(2,1)S(1)}, u32[]{:S(2)}, u32[]{:S(2)}) collective-permute-start(bf16[4,8,8,896]{3,2,1,0:T(8,128)(2,1)} %get-tuple-element.32), channel_id=1, source_target_pairs={{0,24},{8,16},{16,8},{24,0},{1,25},{9,17},{17,9},{25,1},{2,26},{10... | collective-permute-start | bytes 1376264 | tf_op jit(solution)/shard_map/ppermute | solution.py:34
  45.5 28.4 %collective-permute-start.6 = (bf16[4,8,8,896]{3,2,1,0:T(8,128)(2,1)}, bf16[4,8,8,896]{3,2,1,0:T(8,128)(2,1)S(1)}, u32[]{:S(2)}, u32[]{:S(2)}) collective-permute-start(bf16[4,8,8,896]{3,2,1,0:T(8,128)(2,1)} %get-tuple-element.30), channel_id=1, source_target_pairs={{0,8},{8,0},{16,24},{24,16},{1,9},{9,1},{17,25},{25,17},{2,10},{10... | collective-permute-start | bytes 1376264 | tf_op jit(solution)/shard_map/ppermute | solution.py:34
  64.8 35.0 %all-to-all-start.1 = ((bf16[128,8,896]{2,1,0:T(8,128)(2,1)}), bf16[128,8,896]{2,1,0:T(8,128)(2,1)S(1)}, u32[]{:S(2)}, u32[]{:S(2)}) async-start(bf16[128,8,896]{2,1,0:T(8,128)(2,1)} %bitcast.27), calls=%async_computation.1 | async-start | bytes 3670016 | tf_op jit(solution)/shard_map/all_to_all | solution.py:30
  73.3 0.6 copy-start

commit v4 on v3

--- a/solution.py
+++ b/solution.py
@@ -20,7 +20,7 @@
 C6 = 2.0 - 1.25 * C5
 
 TM = ("zlo", "core")
-PLANE = ("x", "zhi", "zlo")
+PLANE = ("x", "zhi", "core")
 BY_ROWS = ("x", "zhi", "mom", "zlo", "core")
 BY_OUTPUT = ("mom", "zlo", "core", "x", "zhi")
 MIB = 1024 * 1024
@@ -42,7 +42,7 @@
         times = [4 * ((place // 4) ^ tm) + place % 4 for place in range(NT)]
         wide.append(np.kron(cosine[:, times], np.eye(16)))
         narrow.append(np.kron(cosine[:, times], np.eye(8)))
-        back.append(np.einsum("tw,cd,ab->ctawdb", cosine[times, :], np.eye(2), np.eye(8)).reshape(256, 256))
+        back.append(np.einsum("tpq,cd,ab->ctapdqb", cosine[times, :].reshape(NT, 8, 2), np.eye(2), np.eye(8)).reshape(256, 256))
     return [np.stack(tables).astype(ml_dtypes.bfloat16) for tables in (wide, narrow, back)]
 
 
@@ -165,7 +165,7 @@
     order = (3, 2, 1, 0)
     targets = [place_ref[1] ^ step for step in order]
     into = [refs[0] if step == 0 else held.at[step - 1] for step in order]
-    reads = start_all([(chi_ref.at[:, target % 2, target // 2], to) for target, to in zip(targets, into)], read)
+    reads = start_all([(chi_ref.at[:, target // 2, target % 2], to) for target, to in zip(targets, into)], read)
     writes = []
     for step, move in zip(order, reads):
         move.wait()

time: 122 us -> 121 us (level)
    all_to_all x2, waiting for transfers between devices: 37.7 us -> 35.1 us  [exchange(): return lax.all_to_all(pieces, axes, split_axis=0, concat_axis=0, tiled=True)]
    ppermute x9, waiting for transfers between devices: 14.1 us -> 15.7 us  [swap(): return lax.ppermute(piece, axes, [(i, i ^ step) for i in range(4)])]
where the time goes in v4:
time: 121 us; the launch traced here: 120 us
  waiting for transfers between devices  50.8 us (42%)
  starting transfers between devices  26.3 us (22%)
  Pallas kernels  21.7 us (18%)
  blocking collectives  15.6 us (13%)
  local copies, waits for them, and re-layouts  4.91 us (4%)
    all_to_all x2, waiting for transfers between devices, exchange(): return lax.all_to_all(pieces, axes, split_axis=0, concat_axis=0, tiled=True)  35.1 us
    ppermute x9, waiting for transfers between devices, swap(): return lax.ppermute(piece, axes, [(i, i ^ step) for i in range(4)])  15.7 us
    all_to_all x1, blocking collectives, exchange(): return lax.all_to_all(pieces, axes, split_axis=0, concat_axis=0, tiled=True)  15.6 us
    all_to_all x2, starting transfers between devices, exchange(): return lax.all_to_all(pieces, axes, split_axis=0, concat_axis=0, tiled=True)  15 us
    ppermute x9, starting transfers between devices, swap(): return lax.ppermute(piece, axes, [(i, i ^ step) for i in range(4)])  11.3 us
    pallas_call x1, Pallas kernels, local(): pl.pallas_call(series_kernel, out_shape=pltpu.HBM((1024, NP), jnp.bfloat1...  7 us
    pallas_call x1, Pallas kernels, local(): pl.pallas_call(self_energy_kernel, out_shape=jax.ShapeDtypeStruct((16, 8,...  5.39 us
    pallas_call x1, Pallas kernels, local(): copies_call(split_rows_kernel, [pltpu.HBM((8, 4, 8, NP), jnp.bfloat16)] *...  2.85 us
  transfers between devices with their start and end apart: 11, of which 6 were waited for; matrix products, arithmetic and copies ran while one was open for 3% of the time, Pallas kernels for 11%

profile of v4, /device:TPU:1, one launch (start us, length us, event | category | flops | bytes accessed | tf_op | source)
XLA Modules:
  0.0 120.3 jit_solution(7120551622888060185)
XLA Ops:
  0.0 0.1 pad_add_fusion.place_ref
  0.1 2.7 %shard_map.64 = (bf16[4,56,896]{2,1,0:T(8,128)(2,1)S(1)}, bf16[4,56,896]{2,1,0:T(8,128)(2,1)}, bf16[4,56,896]{2,1,0:T(8,128)(2,1)}, bf16[4,56,896]{2,1,0:T(8,128)(2,1)}) custom-call(s32[2]{0:T(128)S(1)} %pad_add_fusion.place_ref, bf16[4,2,2,56,896]{4,3,2,1,0:T(8,128)(2,1)} %bitcast.28), custom_call_target="tpu_custom_call" | custom-call | tf_op jit(solution)/shard_map/pallas_call | solution.py:238
  2.8 1.5 %collective-permute-start = (bf16[4,56,896]{2,1,0:T(8,128)(2,1)}, bf16[4,56,896]{2,1,0:T(8,128)(2,1)S(1)}, u32[]{:S(2)}, u32[]{:S(2)}) collective-permute-start(bf16[4,56,896]{2,1,0:T(8,128)(2,1)} %get-tuple-element.21), channel_id=1, source_target_pairs={{0,8},{8,0},{16,24},{24,16},{1,9},{9,1},{17,25},{25,17},{2,10},{10... | collective-permute-start | bytes 1204232 | tf_op jit(solution)/shard_map/ppermute | solution.py:34
  4.3 1.7 %collective-permute-start.1 = (bf16[4,56,896]{2,1,0:T(8,128)(2,1)}, bf16[4,56,896]{2,1,0:T(8,128)(2,1)S(1)}, u32[]{:S(2)}, u32[]{:S(2)}) collective-permute-start(bf16[4,56,896]{2,1,0:T(8,128)(2,1)} %get-tuple-element.22), channel_id=1, source_target_pairs={{0,16},{8,24},{16,0},{24,8},{1,17},{9,25},{17,1},{25,9},{2,18},{10... | collective-permute-start | bytes 1204232 | tf_op jit(solution)/shard_map/ppermute | solution.py:34
  6.0 0.1 collective-permute-start.2
  6.1 2.9 %shard_map.67 = (bf16[8,4,8,896]{3,2,1,0:T(8,128)(2,1)}, bf16[8,4,8,896]{3,2,1,0:T(8,128)(2,1)}, bf16[8,4,8,896]{3,2,1,0:T(8,128)(2,1)}, bf16[8,4,8,896]{3,2,1,0:T(8,128)(2,1)}) custom-call(s32[2]{0:T(128)S(1)} %pad_add_fusion.place_ref, bf16[8,14,8,896]{3,2,1,0:T(8,128)(2,1)} %bitcast.30), custom_call_target="tpu_custom_call" | custom-call | flops 99999997952 | bytes 4194304 | tf_op jit(solution)/shard_map/pallas_call | solution.py:249
  8.9 1.4 %collective-permute-start.3 = (bf16[8,4,8,896]{3,2,1,0:T(8,128)(2,1)}, bf16[8,4,8,896]{3,2,1,0:T(8,128)(2,1)S(1)}, u32[]{:S(2)}, u32[]{:S(2)}) collective-permute-start(bf16[8,4,8,896]{3,2,1,0:T(8,128)(2,1)} %get-tuple-element.26), channel_id=1, source_target_pairs={{0,32},{32,0},{64,96},{96,64},{1,33},{33,1},{65,97},{97,65},{2,34}... | collective-permute-start | bytes 1376264 | tf_op jit(solution)/shard_map/ppermute | solution.py:34
  10.3 2.6 %collective-permute-start.4 = (bf16[8,4,8,896]{3,2,1,0:T(8,128)(2,1)}, bf16[8,4,8,896]{3,2,1,0:T(8,128)(2,1)S(1)}, u32[]{:S(2)}, u32[]{:S(2)}) collective-permute-start(bf16[8,4,8,896]{3,2,1,0:T(8,128)(2,1)} %get-tuple-element.27), channel_id=1, source_target_pairs={{0,64},{32,96},{64,0},{96,32},{1,65},{33,97},{65,1},{97,33},{2,66}... | collective-permute-start | bytes 1376264 | tf_op jit(solution)/shard_map/ppermute | solution.py:34
  12.9 0.8 dynamic-slice_bitcast_fusion.2.narrow_ref
  13.7 0.9 dynamic-slice_bitcast_fusion.1.wide_ref
  14.6 0.1 collective-permute-start.5
  14.7 1.0 collective-permute-done.1.second_ref
  15.8 8.9 %collective-permute-done.2.third_ref = bf16[4,56,896]{2,1,0:T(8,128)(2,1)S(1)} collective-permute-done((bf16[4,56,896]{2,1,0:T(8,128)(2,1)}, bf16[4,56,896]{2,1,0:T(8,128)(2,1)S(1)}, u32[]{:S(2)}, u32[]{:S(2)}) %collective-permute-start.2) | collective-permute-done | bytes 401440 | tf_op jit(solution)/shard_map/ppermute | solution.py:34
  24.7 1.5 %shard_map.65 = bf16[16,56,896]{2,1,0:T(8,128)(2,1)} custom-call(bf16[4,56,896]{2,1,0:T(8,128)(2,1)S(1)} %get-tuple-element.19.own_ref, bf16[4,56,896]{2,1,0:T(8,128)(2,1)S(1)} %collective-permute-done.first_ref, bf16[4,56,896]{2,1,0:T(8,128)(2,1)S(1)} %collective-permute-done.1.second_ref, bf16[4,56,896]{2,1,0:T(8,128)(2,1)S(1)} %collective-permute-done.2.third_ref, ...), custom_call_target="tpu_custom_call" | custom-call | flops 99999997952 | bytes 4194304 | tf_op jit(solution)/shard_map/pallas_call | solution.py:260
  26.2 7.6 %all-to-all-start = ((bf16[16,56,896]{2,1,0:T(8,128)(2,1)}), bf16[16,56,896]{2,1,0:T(8,128)(2,1)S(1)}, u32[]{:S(2)}, u32[]{:S(2)}) async-start(bf16[16,56,896]{2,1,0:T(8,128)(2,1)} %shard_map.65), calls=%async_computation | async-start | bytes 3211264 | tf_op jit(solution)/shard_map/all_to_all | solution.py:30
  33.8 3.3 %collective-permute-done.5.refs_3_ = bf16[8,4,8,896]{3,2,1,0:T(8,128)(2,1)S(1)} collective-permute-done((bf16[8,4,8,896]{3,2,1,0:T(8,128)(2,1)}, bf16[8,4,8,896]{3,2,1,0:T(8,128)(2,1)S(1)}, u32[]{:S(2)}, u32[]{:S(2)}) %collective-permute-start.5) | collective-permute-done | bytes 458784 | tf_op jit(solution)/shard_map/ppermute | solution.py:34
  37.1 1.0 copy-done.1
  38.1 2.3 %shard_map.68 = (bf16[4,8,8,896]{3,2,1,0:T(8,128)(2,1)}, bf16[4,8,8,896]{3,2,1,0:T(8,128)(2,1)}, bf16[4,8,8,896]{3,2,1,0:T(8,128)(2,1)}, bf16[4,8,8,896]{3,2,1,0:T(8,128)(2,1)}) custom-call(s32[2]{0:T(128)S(1)} %pad_add_fusion.place_ref, bf16[8,4,8,896]{3,2,1,0:T(8,128)(2,1)S(1)} %copy-done.1, bf16[8,4,8,896]{3,2,1,0:T(8,128)(2,1)S(1)} %collective-permute-done.3.refs_1_, ...), custom_call_target="tpu_custom_call" | custom-call | flops 99999997952 | bytes 4194304 | tf_op jit(solution)/shard_map/pallas_call | solution.py:268
  40.4 1.9 %collective-permute-start.7 = (bf16[4,8,8,896]{3,2,1,0:T(8,128)(2,1)}, bf16[4,8,8,896]{3,2,1,0:T(8,128)(2,1)S(1)}, u32[]{:S(2)}, u32[]{:S(2)}) collective-permute-start(bf16[4,8,8,896]{3,2,1,0:T(8,128)(2,1)} %get-tuple-element.31), channel_id=1, source_target_pairs={{0,16},{8,24},{16,0},{24,8},{1,17},{9,25},{17,1},{25,9},{2,18},{10... | collective-permute-start | bytes 1376264 | tf_op jit(solution)/shard_map/ppermute | solution.py:34
  42.3 1.6 %collective-permute-start.8 = (bf16[4,8,8,896]{3,2,1,0:T(8,128)(2,1)}, bf16[4,8,8,896]{3,2,1,0:T(8,128)(2,1)S(1)}, u32[]{:S(2)}, u32[]{:S(2)}) collective-permute-start(bf16[4,8,8,896]{3,2,1,0:T(8,128)(2,1)} %get-tuple-element.32), channel_id=1, source_target_pairs={{0,24},{8,16},{16,8},{24,0},{1,25},{9,17},{17,9},{25,1},{2,26},{10... | collective-permute-start | bytes 1376264 | tf_op jit(solution)/shard_map/ppermute | solution.py:34
  43.9 0.7 constant_dynamic-slice_fusion.refs_5_
  44.6 0.9 dynamic-slice_bitcast_fusion.table_ref
  45.5 0.4 collective-permute-start.6
  45.9 11.0 %all-to-all-done = bf16[16,56,896]{2,1,0:T(8,128)(2,1)S(1)} async-done(((bf16[16,56,896]{2,1,0:T(8,128)(2,1)}), bf16[16,56,896]{2,1,0:T(8,128)(2,1)S(1)}, u32[]{:S(2)}, u32[]{:S(2)}) %all-to-all-start) | async-done | bytes 1605664 | tf_op jit(solution)/shard_map/all_to_all | solution.py:30
  56.9 7.0 %shard_map.66 = bf16[1024,896]{1,0:T(8,128)(2,1)} custom-call(bf16[896,896]{1,0:T(8,128)(2,1)S(1)} %bitcast.20), custom_call_target="tpu_custom_call" | custom-call | tf_op jit(solution)/shard_map/pallas_call | solution.py:288
  63.9 7.5 %all-to-all-start.1 = ((bf16[128,8,896]{2,1,0:T(8,128)(2,1)}), bf16[128,8,896]{2,1,0:T(8,128)(2,1)S(1)}, u32[]{:S(2)}, u32[]{:S(2)}) async-start(bf16[128,8,896]{2,1,0:T(8,128)(2,1)} %bitcast.27), calls=%async_computation.1 | async-start | bytes 3670016 | tf_op jit(solution)/shard_map/all_to_all | solution.py:30
  71.4 2.4 %collective-permute-done.8 = bf16[4,8,8,896]{3,2,1,0:T(8,128)(2,1)S(1)} collective-permute-done((bf16[4,8,8,896]{3,2,1,0:T(8,128)(2,1)}, bf16[4,8,8,896]{3,2,1,0:T(8,128)(2,1)S(1)}, u32[]{:S(2)}, u32[]{:S(2)}) %collective-permute-start.8) | collective-permute-done | bytes 458784 | tf_op jit(solution)/shard_map/ppermute | solution.py:34
  73.8 0.6 copy-done
  74.4 24.1 %all-to-all-done.1 = bf16[128,8,896]{2,1,0:T(8,128)(2,1)S(1)} async-done(((bf16[128,8,896]{2,1,0:T(8,128)(2,1)}), bf16[128,8,896]{2,1,0:T(8,128)(2,1)S(1)}, u32[]{:S(2)}, u32[]{:S(2)}) %all-to-all-start.1) | async-done | bytes 1835040 | tf_op jit(solution)/shard_map/all_to_all | solution.py:30
  98.5 5.4 %shard_map.70 = bf16[16,8,8,128]{3,2,1,0:T(8,128)(2,1)S(1)} custom-call(s32[2]{0:T(128)S(1)} %pad_add_fusion.place_ref, bf16[1024,896]{1,0:T(8,128)(2,1)S(1)} %bitcast.19, bf16[256,256]{1,0:T(8,128)(2,1)S(1)} %dynamic-slice_bitcast_fusion.table_ref, bf16[4,64,896]{2,1,0:T(8,128)(2,1)} %bitcast.29, bf16[4,64,896]{2,1,0:T(8,128)(2,1)S(1)} %bitcast.26, ...), custom_call_target="tpu_custom_call" | custom-call | tf_op jit(solution)/shard_map/pallas_call | solution.py:302
  103.9 15.6 %all_to_all.15 = bf16[128,8,128]{2,1,0:T(8,128)(2,1)S(1)} all-to-all(bf16[128,8,128]{2,1,0:T(8,128)(2,1)S(1)} %bitcast.21), channel_id=1, replica_groups=mesh['mom'=4,'zlo'=2,'core'=2,'x'=4,'zhi'=2] {'mom','zlo','core','x','zhi'}, dimensions={0} | all-to-all | bytes 524288 | tf_op jit(solution)/shard_map/all_to_all | solution.py:30
  119.5 0.7 convert_reduce_fusion
  (8 shorter events, 0.0 us)
Async XLA Ops:
  2.8 11.8 %collective-permute-start = (bf16[4,56,896]{2,1,0:T(8,128)(2,1)}, bf16[4,56,896]{2,1,0:T(8,128)(2,1)S(1)}, u32[]{:S(2)}, u32[]{:S(2)}) collective-permute-start(bf16[4,56,896]{2,1,0:T(8,128)(2,1)} %get-tuple-element.21), channel_id=1, source_target_pairs={{0,8},{8,0},{16,24},{24,16},{1,9},{9,1},{17,25},{25,17},{2,10},{10... | collective-permute-start | bytes 1204232 | tf_op jit(solution)/shard_map/ppermute | solution.py:34
  4.3 11.5 %collective-permute-start.1 = (bf16[4,56,896]{2,1,0:T(8,128)(2,1)}, bf16[4,56,896]{2,1,0:T(8,128)(2,1)S(1)}, u32[]{:S(2)}, u32[]{:S(2)}) collective-permute-start(bf16[4,56,896]{2,1,0:T(8,128)(2,1)} %get-tuple-element.22), channel_id=1, source_target_pairs={{0,16},{8,24},{16,0},{24,8},{1,17},{9,25},{17,1},{25,9},{2,18},{10... | collective-permute-start | bytes 1204232 | tf_op jit(solution)/shard_map/ppermute | solution.py:34
  6.0 18.6 %collective-permute-start.2 = (bf16[4,56,896]{2,1,0:T(8,128)(2,1)}, bf16[4,56,896]{2,1,0:T(8,128)(2,1)S(1)}, u32[]{:S(2)}, u32[]{:S(2)}) collective-permute-start(bf16[4,56,896]{2,1,0:T(8,128)(2,1)} %get-tuple-element.23), channel_id=1, source_target_pairs={{0,24},{8,16},{16,8},{24,0},{1,25},{9,17},{17,9},{25,1},{2,26},{10... | collective-permute-start | bytes 1204232 | tf_op jit(solution)/shard_map/ppermute | solution.py:34
  8.9 24.8 %collective-permute-start.3 = (bf16[8,4,8,896]{3,2,1,0:T(8,128)(2,1)}, bf16[8,4,8,896]{3,2,1,0:T(8,128)(2,1)S(1)}, u32[]{:S(2)}, u32[]{:S(2)}) collective-permute-start(bf16[8,4,8,896]{3,2,1,0:T(8,128)(2,1)} %get-tuple-element.26), channel_id=1, source_target_pairs={{0,32},{32,0},{64,96},{96,64},{1,33},{33,1},{65,97},{97,65},{2,34}... | collective-permute-start | bytes 1376264 | tf_op jit(solution)/shard_map/ppermute | solution.py:34
  10.3 23.5 %collective-permute-start.4 = (bf16[8,4,8,896]{3,2,1,0:T(8,128)(2,1)}, bf16[8,4,8,896]{3,2,1,0:T(8,128)(2,1)S(1)}, u32[]{:S(2)}, u32[]{:S(2)}) collective-permute-start(bf16[8,4,8,896]{3,2,1,0:T(8,128)(2,1)} %get-tuple-element.27), channel_id=1, source_target_pairs={{0,64},{32,96},{64,0},{96,32},{1,65},{33,97},{65,1},{97,33},{2,66}... | collective-permute-start | bytes 1376264 | tf_op jit(solution)/shard_map/ppermute | solution.py:34
  14.6 22.5 %collective-permute-start.5 = (bf16[8,4,8,896]{3,2,1,0:T(8,128)(2,1)}, bf16[8,4,8,896]{3,2,1,0:T(8,128)(2,1)S(1)}, u32[]{:S(2)}, u32[]{:S(2)}) collective-permute-start(bf16[8,4,8,896]{3,2,1,0:T(8,128)(2,1)} %get-tuple-element.28), channel_id=1, source_target_pairs={{0,96},{32,64},{64,32},{96,0},{1,97},{33,65},{65,33},{97,1},{2,98}... | collective-permute-start | bytes 1376264 | tf_op jit(solution)/shard_map/ppermute | solution.py:34
  26.2 30.8 %all-to-all-start = ((bf16[16,56,896]{2,1,0:T(8,128)(2,1)}), bf16[16,56,896]{2,1,0:T(8,128)(2,1)S(1)}, u32[]{:S(2)}, u32[]{:S(2)}) async-start(bf16[16,56,896]{2,1,0:T(8,128)(2,1)} %shard_map.65), calls=%async_computation | async-start | bytes 3211264 | tf_op jit(solution)/shard_map/all_to_all | solution.py:30
  37.1 1.0 copy-start.1
  40.4 31.0 %collective-permute-start.7 = (bf16[4,8,8,896]{3,2,1,0:T(8,128)(2,1)}, bf16[4,8,8,896]{3,2,1,0:T(8,128)(2,1)S(1)}, u32[]{:S(2)}, u32[]{:S(2)}) collective-permute-start(bf16[4,8,8,896]{3,2,1,0:T(8,128)(2,1)} %get-tuple-element.31), channel_id=1, source_target_pairs={{0,16},{8,24},{16,0},{24,8},{1,17},{9,25},{17,1},{25,9},{2,18},{10... | collective-permute-start | bytes 1376264 | tf_op jit(solution)/shard_map/ppermute | solution.py:34
  42.3 31.5 %collective-permute-start.8 = (bf16[4,8,8,896]{3,2,1,0:T(8,128)(2,1)}, bf16[4,8,8,896]{3,2,1,0:T(8,128)(2,1)S(1)}, u32[]{:S(2)}, u32[]{:S(2)}) collective-permute-start(bf16[4,8,8,896]{3,2,1,0:T(8,128)(2,1)} %get-tuple-element.32), channel_id=1, source_target_pairs={{0,24},{8,16},{16,8},{24,0},{1,25},{9,17},{17,9},{25,1},{2,26},{10... | collective-permute-start | bytes 1376264 | tf_op jit(solution)/shard_map/ppermute | solution.py:34
  45.5 28.9 %collective-permute-start.6 = (bf16[4,8,8,896]{3,2,1,0:T(8,128)(2,1)}, bf16[4,8,8,896]{3,2,1,0:T(8,128)(2,1)S(1)}, u32[]{:S(2)}, u32[]{:S(2)}) collective-permute-start(bf16[4,8,8,896]{3,2,1,0:T(8,128)(2,1)} %get-tuple-element.30), channel_id=1, source_target_pairs={{0,8},{8,0},{16,24},{24,16},{1,9},{9,1},{17,25},{25,17},{2,10},{10... | collective-permute-start | bytes 1376264 | tf_op jit(solution)/shard_map/ppermute | solution.py:34
  63.9 34.6 %all-to-all-start.1 = ((bf16[128,8,896]{2,1,0:T(8,128)(2,1)}), bf16[128,8,896]{2,1,0:T(8,128)(2,1)S(1)}, u32[]{:S(2)}, u32[]{:S(2)}) async-start(bf16[128,8,896]{2,1,0:T(8,128)(2,1)} %bitcast.27), calls=%async_computation.1 | async-start | bytes 3670016 | tf_op jit(solution)/shard_map/all_to_all | solution.py:30
  73.8 0.6 copy-start

commit v5 on v4

--- a/solution.py
+++ b/solution.py
@@ -63,7 +63,7 @@
 
 
 def series_kernel(tile_ref, out_ref, square_ref, sum_ref, fourth_ref, left_ref, right_ref, padded_ref, sent):
-    step = 224
+    step = 448
     for at in range(0, NP, step):
         rows = slice(at, at + step)
         square = jnp.dot(tile_ref[rows, :], tile_ref[...], preferred_element_type=jnp.float32).astype(jnp.bfloat16)
@@ -78,7 +78,7 @@
         right_ref[rows, :] = (fourth + C5 * square).astype(jnp.bfloat16)
         fourth_ref[rows, :] = C6 * fourth + square + tile
     sends = []
-    for at, count in (0, 224), (224, 224), (448, 224), (672, 112), (784, 112):
+    for at, count in (0, 448), (448, 224), (672, 112), (784, 112):
         rows = slice(at, at + count)
         total = jnp.dot(left_ref[rows, :], right_ref[...], preferred_element_type=jnp.float32) + fourth_ref[rows, :]
         total = total.astype(jnp.bfloat16)
@@ -291,7 +291,7 @@
         out_specs=HBM,
         scratch_shapes=[square, square, pltpu.VMEM((NP, NP), jnp.float32), square, square]
         + [pltpu.VMEM((1024, NP), jnp.bfloat16), sems(5)],
-        compiler_params=vmem(16),
+        compiler_params=vmem(22),
         cost_estimate=None,
     )(tile)
     spread = exchange(screened.reshape(128, 8, NP), BY_ROWS).reshape(1024, NP)

time: 121 us -> 121 us (level)
  no operation moved by 1% of the time
where the time goes in v5:
time: 121 us; the launch traced here: 120 us
  waiting for transfers between devices  50.8 us (42%)
  starting transfers between devices  26.3 us (22%)
  Pallas kernels  21.6 us (18%)
  blocking collectives  15.6 us (13%)
  local copies, waits for them, and re-layouts  4.91 us (4%)
    all_to_all x2, waiting for transfers between devices, exchange(): return lax.all_to_all(pieces, axes, split_axis=0, concat_axis=0, tiled=True)  35.1 us
    ppermute x9, waiting for transfers between devices, swap(): return lax.ppermute(piece, axes, [(i, i ^ step) for i in range(4)])  15.7 us
    all_to_all x1, blocking collectives, exchange(): return lax.all_to_all(pieces, axes, split_axis=0, concat_axis=0, tiled=True)  15.6 us
    all_to_all x2, starting transfers between devices, exchange(): return lax.all_to_all(pieces, axes, split_axis=0, concat_axis=0, tiled=True)  15 us
    ppermute x9, starting transfers between devices, swap(): return lax.ppermute(piece, axes, [(i, i ^ step) for i in range(4)])  11.3 us
    pallas_call x1, Pallas kernels, local(): pl.pallas_call(series_kernel, out_shape=pltpu.HBM((1024, NP), jnp.bfloat1...  6.93 us
    pallas_call x1, Pallas kernels, local(): pl.pallas_call(self_energy_kernel, out_shape=jax.ShapeDtypeStruct((16, 8,...  5.39 us
    pallas_call x1, Pallas kernels, local(): copies_call(split_rows_kernel, [pltpu.HBM((8, 4, 8, NP), jnp.bfloat16)] *...  2.85 us
  transfers between devices with their start and end apart: 11, of which 6 were waited for; matrix products, arithmetic and copies ran while one was open for 3% of the time, Pallas kernels for 11%

profile of v5, /device:TPU:1, one launch (start us, length us, event | category | flops | bytes accessed | tf_op | source)
XLA Modules:
  0.0 120.2 jit_solution(16641860076452367979)
XLA Ops:
  0.0 0.1 pad_add_fusion.place_ref
  0.1 2.7 %shard_map.64 = (bf16[4,56,896]{2,1,0:T(8,128)(2,1)S(1)}, bf16[4,56,896]{2,1,0:T(8,128)(2,1)}, bf16[4,56,896]{2,1,0:T(8,128)(2,1)}, bf16[4,56,896]{2,1,0:T(8,128)(2,1)}) custom-call(s32[2]{0:T(128)S(1)} %pad_add_fusion.place_ref, bf16[4,2,2,56,896]{4,3,2,1,0:T(8,128)(2,1)} %bitcast.28), custom_call_target="tpu_custom_call" | custom-call | tf_op jit(solution)/shard_map/pallas_call | solution.py:238
  2.8 1.5 %collective-permute-start = (bf16[4,56,896]{2,1,0:T(8,128)(2,1)}, bf16[4,56,896]{2,1,0:T(8,128)(2,1)S(1)}, u32[]{:S(2)}, u32[]{:S(2)}) collective-permute-start(bf16[4,56,896]{2,1,0:T(8,128)(2,1)} %get-tuple-element.21), channel_id=1, source_target_pairs={{0,8},{8,0},{16,24},{24,16},{1,9},{9,1},{17,25},{25,17},{2,10},{10... | collective-permute-start | bytes 1204232 | tf_op jit(solution)/shard_map/ppermute | solution.py:34
  4.3 1.7 %collective-permute-start.1 = (bf16[4,56,896]{2,1,0:T(8,128)(2,1)}, bf16[4,56,896]{2,1,0:T(8,128)(2,1)S(1)}, u32[]{:S(2)}, u32[]{:S(2)}) collective-permute-start(bf16[4,56,896]{2,1,0:T(8,128)(2,1)} %get-tuple-element.22), channel_id=1, source_target_pairs={{0,16},{8,24},{16,0},{24,8},{1,17},{9,25},{17,1},{25,9},{2,18},{10... | collective-permute-start | bytes 1204232 | tf_op jit(solution)/shard_map/ppermute | solution.py:34
  6.0 0.1 collective-permute-start.2
  6.1 2.9 %shard_map.67 = (bf16[8,4,8,896]{3,2,1,0:T(8,128)(2,1)}, bf16[8,4,8,896]{3,2,1,0:T(8,128)(2,1)}, bf16[8,4,8,896]{3,2,1,0:T(8,128)(2,1)}, bf16[8,4,8,896]{3,2,1,0:T(8,128)(2,1)}) custom-call(s32[2]{0:T(128)S(1)} %pad_add_fusion.place_ref, bf16[8,14,8,896]{3,2,1,0:T(8,128)(2,1)} %bitcast.30), custom_call_target="tpu_custom_call" | custom-call | flops 99999997952 | bytes 4194304 | tf_op jit(solution)/shard_map/pallas_call | solution.py:249
  8.9 1.4 %collective-permute-start.3 = (bf16[8,4,8,896]{3,2,1,0:T(8,128)(2,1)}, bf16[8,4,8,896]{3,2,1,0:T(8,128)(2,1)S(1)}, u32[]{:S(2)}, u32[]{:S(2)}) collective-permute-start(bf16[8,4,8,896]{3,2,1,0:T(8,128)(2,1)} %get-tuple-element.26), channel_id=1, source_target_pairs={{0,32},{32,0},{64,96},{96,64},{1,33},{33,1},{65,97},{97,65},{2,34}... | collective-permute-start | bytes 1376264 | tf_op jit(solution)/shard_map/ppermute | solution.py:34
  10.3 2.6 %collective-permute-start.4 = (bf16[8,4,8,896]{3,2,1,0:T(8,128)(2,1)}, bf16[8,4,8,896]{3,2,1,0:T(8,128)(2,1)S(1)}, u32[]{:S(2)}, u32[]{:S(2)}) collective-permute-start(bf16[8,4,8,896]{3,2,1,0:T(8,128)(2,1)} %get-tuple-element.27), channel_id=1, source_target_pairs={{0,64},{32,96},{64,0},{96,32},{1,65},{33,97},{65,1},{97,33},{2,66}... | collective-permute-start | bytes 1376264 | tf_op jit(solution)/shard_map/ppermute | solution.py:34
  12.9 0.8 dynamic-slice_bitcast_fusion.2.narrow_ref
  13.7 0.9 dynamic-slice_bitcast_fusion.1.wide_ref
  14.6 0.1 collective-permute-start.5
  14.7 1.0 collective-permute-done.1.second_ref
  15.8 8.9 %collective-permute-done.2.third_ref = bf16[4,56,896]{2,1,0:T(8,128)(2,1)S(1)} collective-permute-done((bf16[4,56,896]{2,1,0:T(8,128)(2,1)}, bf16[4,56,896]{2,1,0:T(8,128)(2,1)S(1)}, u32[]{:S(2)}, u32[]{:S(2)}) %collective-permute-start.2) | collective-permute-done | bytes 401440 | tf_op jit(solution)/shard_map/ppermute | solution.py:34
  24.7 1.5 %shard_map.65 = bf16[16,56,896]{2,1,0:T(8,128)(2,1)} custom-call(bf16[4,56,896]{2,1,0:T(8,128)(2,1)S(1)} %get-tuple-element.19.own_ref, bf16[4,56,896]{2,1,0:T(8,128)(2,1)S(1)} %collective-permute-done.first_ref, bf16[4,56,896]{2,1,0:T(8,128)(2,1)S(1)} %collective-permute-done.1.second_ref, bf16[4,56,896]{2,1,0:T(8,128)(2,1)S(1)} %collective-permute-done.2.third_ref, ...), custom_call_target="tpu_custom_call" | custom-call | flops 99999997952 | bytes 4194304 | tf_op jit(solution)/shard_map/pallas_call | solution.py:260
  26.2 7.6 %all-to-all-start = ((bf16[16,56,896]{2,1,0:T(8,128)(2,1)}), bf16[16,56,896]{2,1,0:T(8,128)(2,1)S(1)}, u32[]{:S(2)}, u32[]{:S(2)}) async-start(bf16[16,56,896]{2,1,0:T(8,128)(2,1)} %shard_map.65), calls=%async_computation | async-start | bytes 3211264 | tf_op jit(solution)/shard_map/all_to_all | solution.py:30
  33.8 3.3 %collective-permute-done.5.refs_3_ = bf16[8,4,8,896]{3,2,1,0:T(8,128)(2,1)S(1)} collective-permute-done((bf16[8,4,8,896]{3,2,1,0:T(8,128)(2,1)}, bf16[8,4,8,896]{3,2,1,0:T(8,128)(2,1)S(1)}, u32[]{:S(2)}, u32[]{:S(2)}) %collective-permute-start.5) | collective-permute-done | bytes 458784 | tf_op jit(solution)/shard_map/ppermute | solution.py:34
  37.1 1.0 copy-done.1
  38.1 2.3 %shard_map.68 = (bf16[4,8,8,896]{3,2,1,0:T(8,128)(2,1)}, bf16[4,8,8,896]{3,2,1,0:T(8,128)(2,1)}, bf16[4,8,8,896]{3,2,1,0:T(8,128)(2,1)}, bf16[4,8,8,896]{3,2,1,0:T(8,128)(2,1)}) custom-call(s32[2]{0:T(128)S(1)} %pad_add_fusion.place_ref, bf16[8,4,8,896]{3,2,1,0:T(8,128)(2,1)S(1)} %copy-done.1, bf16[8,4,8,896]{3,2,1,0:T(8,128)(2,1)S(1)} %collective-permute-done.3.refs_1_, ...), custom_call_target="tpu_custom_call" | custom-call | flops 99999997952 | bytes 4194304 | tf_op jit(solution)/shard_map/pallas_call | solution.py:268
  40.4 1.9 %collective-permute-start.7 = (bf16[4,8,8,896]{3,2,1,0:T(8,128)(2,1)}, bf16[4,8,8,896]{3,2,1,0:T(8,128)(2,1)S(1)}, u32[]{:S(2)}, u32[]{:S(2)}) collective-permute-start(bf16[4,8,8,896]{3,2,1,0:T(8,128)(2,1)} %get-tuple-element.31), channel_id=1, source_target_pairs={{0,16},{8,24},{16,0},{24,8},{1,17},{9,25},{17,1},{25,9},{2,18},{10... | collective-permute-start | bytes 1376264 | tf_op jit(solution)/shard_map/ppermute | solution.py:34
  42.3 1.6 %collective-permute-start.8 = (bf16[4,8,8,896]{3,2,1,0:T(8,128)(2,1)}, bf16[4,8,8,896]{3,2,1,0:T(8,128)(2,1)S(1)}, u32[]{:S(2)}, u32[]{:S(2)}) collective-permute-start(bf16[4,8,8,896]{3,2,1,0:T(8,128)(2,1)} %get-tuple-element.32), channel_id=1, source_target_pairs={{0,24},{8,16},{16,8},{24,0},{1,25},{9,17},{17,9},{25,1},{2,26},{10... | collective-permute-start | bytes 1376264 | tf_op jit(solution)/shard_map/ppermute | solution.py:34
  43.9 0.7 constant_dynamic-slice_fusion.refs_5_
  44.6 0.9 dynamic-slice_bitcast_fusion.table_ref
  45.5 0.4 collective-permute-start.6
  45.9 11.0 %all-to-all-done = bf16[16,56,896]{2,1,0:T(8,128)(2,1)S(1)} async-done(((bf16[16,56,896]{2,1,0:T(8,128)(2,1)}), bf16[16,56,896]{2,1,0:T(8,128)(2,1)S(1)}, u32[]{:S(2)}, u32[]{:S(2)}) %all-to-all-start) | async-done | bytes 1605664 | tf_op jit(solution)/shard_map/all_to_all | solution.py:30
  56.9 6.9 %shard_map.66 = bf16[1024,896]{1,0:T(8,128)(2,1)} custom-call(bf16[896,896]{1,0:T(8,128)(2,1)S(1)} %bitcast.20), custom_call_target="tpu_custom_call" | custom-call | tf_op jit(solution)/shard_map/pallas_call | solution.py:288
  63.9 7.5 %all-to-all-start.1 = ((bf16[128,8,896]{2,1,0:T(8,128)(2,1)}), bf16[128,8,896]{2,1,0:T(8,128)(2,1)S(1)}, u32[]{:S(2)}, u32[]{:S(2)}) async-start(bf16[128,8,896]{2,1,0:T(8,128)(2,1)} %bitcast.27), calls=%async_computation.1 | async-start | bytes 3670016 | tf_op jit(solution)/shard_map/all_to_all | solution.py:30
  71.4 2.5 %collective-permute-done.8 = bf16[4,8,8,896]{3,2,1,0:T(8,128)(2,1)S(1)} collective-permute-done((bf16[4,8,8,896]{3,2,1,0:T(8,128)(2,1)}, bf16[4,8,8,896]{3,2,1,0:T(8,128)(2,1)S(1)}, u32[]{:S(2)}, u32[]{:S(2)}) %collective-permute-start.8) | collective-permute-done | bytes 458784 | tf_op jit(solution)/shard_map/ppermute | solution.py:34
  73.8 0.6 copy-done
  74.4 24.0 %all-to-all-done.1 = bf16[128,8,896]{2,1,0:T(8,128)(2,1)S(1)} async-done(((bf16[128,8,896]{2,1,0:T(8,128)(2,1)}), bf16[128,8,896]{2,1,0:T(8,128)(2,1)S(1)}, u32[]{:S(2)}, u32[]{:S(2)}) %all-to-all-start.1) | async-done | bytes 1835040 | tf_op jit(solution)/shard_map/all_to_all | solution.py:30
  98.5 5.4 %shard_map.70 = bf16[16,8,8,128]{3,2,1,0:T(8,128)(2,1)S(1)} custom-call(s32[2]{0:T(128)S(1)} %pad_add_fusion.place_ref, bf16[1024,896]{1,0:T(8,128)(2,1)S(1)} %bitcast.19, bf16[256,256]{1,0:T(8,128)(2,1)S(1)} %dynamic-slice_bitcast_fusion.table_ref, bf16[4,64,896]{2,1,0:T(8,128)(2,1)} %bitcast.29, bf16[4,64,896]{2,1,0:T(8,128)(2,1)S(1)} %bitcast.26, ...), custom_call_target="tpu_custom_call" | custom-call | tf_op jit(solution)/shard_map/pallas_call | solution.py:302
  103.9 15.6 %all_to_all.15 = bf16[128,8,128]{2,1,0:T(8,128)(2,1)S(1)} all-to-all(bf16[128,8,128]{2,1,0:T(8,128)(2,1)S(1)} %bitcast.21), channel_id=1, replica_groups=mesh['mom'=4,'zlo'=2,'core'=2,'x'=4,'zhi'=2] {'mom','zlo','core','x','zhi'}, dimensions={0} | all-to-all | bytes 524288 | tf_op jit(solution)/shard_map/all_to_all | solution.py:30
  119.5 0.7 convert_reduce_fusion
  (8 shorter events, 0.0 us)
Async XLA Ops:
  2.8 11.8 %collective-permute-start = (bf16[4,56,896]{2,1,0:T(8,128)(2,1)}, bf16[4,56,896]{2,1,0:T(8,128)(2,1)S(1)}, u32[]{:S(2)}, u32[]{:S(2)}) collective-permute-start(bf16[4,56,896]{2,1,0:T(8,128)(2,1)} %get-tuple-element.21), channel_id=1, source_target_pairs={{0,8},{8,0},{16,24},{24,16},{1,9},{9,1},{17,25},{25,17},{2,10},{10... | collective-permute-start | bytes 1204232 | tf_op jit(solution)/shard_map/ppermute | solution.py:34
  4.3 11.5 %collective-permute-start.1 = (bf16[4,56,896]{2,1,0:T(8,128)(2,1)}, bf16[4,56,896]{2,1,0:T(8,128)(2,1)S(1)}, u32[]{:S(2)}, u32[]{:S(2)}) collective-permute-start(bf16[4,56,896]{2,1,0:T(8,128)(2,1)} %get-tuple-element.22), channel_id=1, source_target_pairs={{0,16},{8,24},{16,0},{24,8},{1,17},{9,25},{17,1},{25,9},{2,18},{10... | collective-permute-start | bytes 1204232 | tf_op jit(solution)/shard_map/ppermute | solution.py:34
  6.0 18.6 %collective-permute-start.2 = (bf16[4,56,896]{2,1,0:T(8,128)(2,1)}, bf16[4,56,896]{2,1,0:T(8,128)(2,1)S(1)}, u32[]{:S(2)}, u32[]{:S(2)}) collective-permute-start(bf16[4,56,896]{2,1,0:T(8,128)(2,1)} %get-tuple-element.23), channel_id=1, source_target_pairs={{0,24},{8,16},{16,8},{24,0},{1,25},{9,17},{17,9},{25,1},{2,26},{10... | collective-permute-start | bytes 1204232 | tf_op jit(solution)/shard_map/ppermute | solution.py:34
  8.9 24.8 %collective-permute-start.3 = (bf16[8,4,8,896]{3,2,1,0:T(8,128)(2,1)}, bf16[8,4,8,896]{3,2,1,0:T(8,128)(2,1)S(1)}, u32[]{:S(2)}, u32[]{:S(2)}) collective-permute-start(bf16[8,4,8,896]{3,2,1,0:T(8,128)(2,1)} %get-tuple-element.26), channel_id=1, source_target_pairs={{0,32},{32,0},{64,96},{96,64},{1,33},{33,1},{65,97},{97,65},{2,34}... | collective-permute-start | bytes 1376264 | tf_op jit(solution)/shard_map/ppermute | solution.py:34
  10.3 23.5 %collective-permute-start.4 = (bf16[8,4,8,896]{3,2,1,0:T(8,128)(2,1)}, bf16[8,4,8,896]{3,2,1,0:T(8,128)(2,1)S(1)}, u32[]{:S(2)}, u32[]{:S(2)}) collective-permute-start(bf16[8,4,8,896]{3,2,1,0:T(8,128)(2,1)} %get-tuple-element.27), channel_id=1, source_target_pairs={{0,64},{32,96},{64,0},{96,32},{1,65},{33,97},{65,1},{97,33},{2,66}... | collective-permute-start | bytes 1376264 | tf_op jit(solution)/shard_map/ppermute | solution.py:34
  14.6 22.5 %collective-permute-start.5 = (bf16[8,4,8,896]{3,2,1,0:T(8,128)(2,1)}, bf16[8,4,8,896]{3,2,1,0:T(8,128)(2,1)S(1)}, u32[]{:S(2)}, u32[]{:S(2)}) collective-permute-start(bf16[8,4,8,896]{3,2,1,0:T(8,128)(2,1)} %get-tuple-element.28), channel_id=1, source_target_pairs={{0,96},{32,64},{64,32},{96,0},{1,97},{33,65},{65,33},{97,1},{2,98}... | collective-permute-start | bytes 1376264 | tf_op jit(solution)/shard_map/ppermute | solution.py:34
  26.2 30.8 %all-to-all-start = ((bf16[16,56,896]{2,1,0:T(8,128)(2,1)}), bf16[16,56,896]{2,1,0:T(8,128)(2,1)S(1)}, u32[]{:S(2)}, u32[]{:S(2)}) async-start(bf16[16,56,896]{2,1,0:T(8,128)(2,1)} %shard_map.65), calls=%async_computation | async-start | bytes 3211264 | tf_op jit(solution)/shard_map/all_to_all | solution.py:30
  37.1 1.0 copy-start.1
  40.4 31.0 %collective-permute-start.7 = (bf16[4,8,8,896]{3,2,1,0:T(8,128)(2,1)}, bf16[4,8,8,896]{3,2,1,0:T(8,128)(2,1)S(1)}, u32[]{:S(2)}, u32[]{:S(2)}) collective-permute-start(bf16[4,8,8,896]{3,2,1,0:T(8,128)(2,1)} %get-tuple-element.31), channel_id=1, source_target_pairs={{0,16},{8,24},{16,0},{24,8},{1,17},{9,25},{17,1},{25,9},{2,18},{10... | collective-permute-start | bytes 1376264 | tf_op jit(solution)/shard_map/ppermute | solution.py:34
  42.3 31.5 %collective-permute-start.8 = (bf16[4,8,8,896]{3,2,1,0:T(8,128)(2,1)}, bf16[4,8,8,896]{3,2,1,0:T(8,128)(2,1)S(1)}, u32[]{:S(2)}, u32[]{:S(2)}) collective-permute-start(bf16[4,8,8,896]{3,2,1,0:T(8,128)(2,1)} %get-tuple-element.32), channel_id=1, source_target_pairs={{0,24},{8,16},{16,8},{24,0},{1,25},{9,17},{17,9},{25,1},{2,26},{10... | collective-permute-start | bytes 1376264 | tf_op jit(solution)/shard_map/ppermute | solution.py:34
  45.5 28.9 %collective-permute-start.6 = (bf16[4,8,8,896]{3,2,1,0:T(8,128)(2,1)}, bf16[4,8,8,896]{3,2,1,0:T(8,128)(2,1)S(1)}, u32[]{:S(2)}, u32[]{:S(2)}) collective-permute-start(bf16[4,8,8,896]{3,2,1,0:T(8,128)(2,1)} %get-tuple-element.30), channel_id=1, source_target_pairs={{0,8},{8,0},{16,24},{24,16},{1,9},{9,1},{17,25},{25,17},{2,10},{10... | collective-permute-start | bytes 1376264 | tf_op jit(solution)/shard_map/ppermute | solution.py:34
  63.9 34.6 %all-to-all-start.1 = ((bf16[128,8,896]{2,1,0:T(8,128)(2,1)}), bf16[128,8,896]{2,1,0:T(8,128)(2,1)S(1)}, u32[]{:S(2)}, u32[]{:S(2)}) async-start(bf16[128,8,896]{2,1,0:T(8,128)(2,1)} %bitcast.27), calls=%async_computation.1 | async-start | bytes 3670016 | tf_op jit(solution)/shard_map/all_to_all | solution.py:30
  73.8 0.6 copy-start
